TPU v7x, 256 devices: a whole 4x4x8 slice. The times are simulated.
256 devices in a mesh: space: 64 (over x, z, core), slab: 4 (over y).
Axes of the slice: x: 4, y: 4, z: 8, core: 2. Of those that a mesh axis runs over, the one named last changes fastest.
Arguments:
- tokens: float32 [65536, 512], P(('space', 'slab')), may hold values from -6 to 6
- gain: float32 [512], replicated, may hold values from 0.25 to 1.75
- query_weight: float32 [512, 512], replicated, may hold values from -3.1 to 3.1
- key_weight: float32 [512, 512], replicated, may hold values from -0.25 to 0.25
- value_weight: float32 [512, 512], replicated, may hold values from -0.25 to 0.25
- output_weight: float32 [512, 512], replicated, may hold values from -0.25 to 0.25
- neighbour_list: int32 [512, 3], P(('space', 'slab')), may hold values from 0 to 5, as said below
- neighbour_count: int32 [512], P(('space', 'slab')), may hold values from 1 to 3, as said below
- cotangent: float32 [65536, 512], P(('space', 'slab')), may hold values from -6 to 6
Outputs:
- result: float32 [65536, 512], P(('space', 'slab'))
- d_tokens: float32 [65536, 512], P(('space', 'slab'))
- d_gain: float32 [512], replicated
- d_query: float32 [512, 512], replicated
- d_key: float32 [512, 512], replicated
- d_value: float32 [512, 512], replicated
- d_output: float32 [512, 512], replicated
Inputs may be any that keep to these rules, and one draw needn't show every extreme that they name: `neighbour_list`: each row holds distinct window indices, never the patch's own index 2 + p % 2. Only the first neighbour_count[p] entries of a row are live.
All inputs are finite; a program needn't handle non-finite values.
Results may differ from a plain program's by a relative error of at most 0.0003.
Values sent between devices are 32-bit elements; how exact they have to be, the bound alone decides.
A program may use at most 128 MiB of HBM per device.

v0:
```python
import jax
import jax.numpy as jnp
from jax import lax
from jax.sharding import PartitionSpec as P

HEADS = 8
PT = 128


def extended(cells, sides, width):
    for axis, dim in sides:
        count = lax.axis_size(axis)
        head = lax.slice_in_dim(cells, 0, width, axis=dim)
        tail = lax.slice_in_dim(cells, cells.shape[dim] - width, cells.shape[dim], axis=dim)
        cells = jnp.concatenate(
            [
                lax.ppermute(tail, axis, [(i, (i + 1) % count) for i in range(count)]),
                cells,
                lax.ppermute(head, axis, [((i + 1) % count, i) for i in range(count)]),
            ],
            axis=dim,
        )
    return cells


def passed_along(value, axis, steps):
    count = lax.axis_size(axis)
    pairs = [(source, (source + steps) % count) for source in range(count)]
    return lax.ppermute(value, axis, pairs)


def matmul(left, right):
    return jnp.dot(left, right, precision=lax.Precision.HIGHEST, preferred_element_type=jnp.float32)


def normalize(tokens, gain):
    row_mean = jnp.mean(tokens, axis=1, keepdims=True)
    centred = tokens - row_mean
    variance = jnp.mean(centred * centred, axis=1, keepdims=True)
    return centred * lax.rsqrt(variance + 1e-05) * gain[None, :]


def attention(query, key_win, value_win, block_index, live_mask):
    patch_count = block_index.shape[0]
    model_width = query.shape[1]
    head_dim = model_width // HEADS
    picked_keys = key_win.reshape(-1, PT, model_width)[block_index].reshape(
        patch_count, -1, HEADS, head_dim
    )
    picked_values = value_win.reshape(-1, PT, model_width)[block_index].reshape(
        patch_count, -1, HEADS, head_dim
    )
    query_blocks = query.reshape(patch_count, PT, HEADS, head_dim)
    scores = jnp.einsum(
        "pqhd,pkhd->phqk", query_blocks, picked_keys, precision=lax.Precision.HIGHEST
    ) * head_dim ** (-0.5)
    key_mask = jnp.repeat(live_mask, PT, axis=1)
    scores = jnp.where(key_mask[:, None, None, :], scores, -1e30)
    row_max = jnp.max(scores, axis=3, keepdims=True)
    weights = jnp.exp(scores - row_max)
    probability = weights / jnp.sum(weights, axis=3, keepdims=True)
    mixed = jnp.einsum(
        "phqk,pkhd->pqhd", probability, picked_values, precision=lax.Precision.HIGHEST
    )
    return mixed.reshape(patch_count * PT, model_width)


def body(
    tokens,
    gain,
    query_weight,
    key_weight,
    value_weight,
    output_weight,
    neighbour_list,
    neighbour_count,
    cotangent,
):
    row_count = tokens.shape[0]
    model_width = tokens.shape[1]
    patch_count = neighbour_list.shape[0]
    hidden, norm_pull = jax.vjp(normalize, tokens, gain)
    query = matmul(hidden, query_weight)
    own_blocks = patch_count + jnp.arange(patch_count, dtype=jnp.int32)
    block_index = jnp.concatenate([own_blocks[:, None], neighbour_list], axis=1)
    slot_ids = jnp.arange(neighbour_list.shape[1], dtype=jnp.int32)
    live_mask = jnp.concatenate(
        [jnp.ones((patch_count, 1), dtype=bool), slot_ids[None, :] < neighbour_count[:, None]],
        axis=1,
    )
    key_rows = matmul(hidden, key_weight)
    value_rows = matmul(hidden, value_weight)
    window = extended(jnp.concatenate([key_rows, value_rows], axis=1), (("space", 0),), row_count)
    key_win = window[:, :model_width]
    value_win = window[:, model_width:]

    def local_attention(query_rows, key_part, value_part):
        return attention(query_rows, key_part, value_part, block_index, live_mask)

    mixed, attention_pull = jax.vjp(local_attention, query, key_win, value_win)
    result = matmul(mixed, output_weight) + tokens
    grad_output = matmul(mixed.T, cotangent)
    d_mixed = matmul(cotangent, output_weight.T)
    d_queries, d_key_win, d_value_win = attention_pull(d_mixed)
    grad_query = matmul(hidden.T, d_queries)
    d_window = jnp.concatenate([d_key_win, d_value_win], axis=1)
    d_owned = d_window[row_count : 2 * row_count]
    for offset, halo_part in ((-1, d_window[:row_count]), (1, d_window[2 * row_count :])):
        d_owned = d_owned + passed_along(halo_part, "space", offset)
    d_keys = d_owned[:, :model_width]
    d_values = d_owned[:, model_width:]
    grad_key = matmul(hidden.T, d_keys)
    grad_value = matmul(hidden.T, d_values)
    d_hidden = (
        matmul(d_queries, query_weight.T)
        + matmul(d_keys, key_weight.T)
        + matmul(d_values, value_weight.T)
    )
    d_norm, grad_gain = norm_pull(d_hidden)
    d_tokens = d_norm + cotangent
    grad_gain, grad_query, grad_key, grad_value, grad_output = lax.psum(
        (grad_gain, grad_query, grad_key, grad_value, grad_output), ("space", "slab")
    )
    return (result, d_tokens, grad_gain, grad_query, grad_key, grad_value, grad_output)


def solution(mesh):
    return jax.shard_map(
        body,
        mesh=mesh,
        in_specs=(
            P(("space", "slab"), None),
            P(),
            P(),
            P(),
            P(),
            P(),
            P(("space", "slab"), None),
            P(("space", "slab")),
            P(("space", "slab"), None),
        ),
        out_specs=(P(("space", "slab"), None), P(("space", "slab"), None), P(), P(), P(), P(), P()),
        check_vma=False,
    )
```

profile of v0, /device:TPU:1, one launch (start us, length us, event | category | flops | bytes accessed | tf_op | source)
XLA Modules:
  0.0 427.9 jit_solution(7895990466346102938)
XLA Ops:
  7.3 1.3 reduce_sum.78
  9.8 2.2 fusion.56
  12.0 2.6 fusion.57
  15.6 3.2 collective-permute-start.1
  19.4 3.9 fusion.55
  23.3 2.1 reshape.174
  25.4 3.0 fusion.62
  28.4 2.1 reshape.178
  31.7 1.9 pad_maximum_fusion
  33.6 1.5 fusion.61
  35.1 3.4 gather_fusion
  38.5 4.9 %reshape.226 = f32[2,512,8,64]{3,2,1,0:T(8,128)} reshape(f32[8,128,512]{2,1,0:T(8,128)} %gather_fusion) | data formatting | bytes 4194304 | tf_op jit(solution)/shard_map/jvp()/reshape | solution.py:50
  43.4 3.8 copy.41
  47.2 2.0 gather_fusion.1
  49.2 4.4 %reshape.227 = f32[2,512,8,64]{3,2,1,0:T(8,128)} reshape(f32[8,128,512]{2,1,0:T(8,128)} %gather_fusion.1) | data formatting | bytes 4194304 | tf_op jit(solution)/shard_map/jvp()/reshape | solution.py:47
  53.6 3.9 copy.40
  57.5 5.7 %fusion.1 = (f32[2,8,128]{2,1,0:T(8,128)S(1)}, f32[2,8,128,512]{3,2,1,0:T(8,128)S(1)}) fusion(pred[2,512]{1,0:T(4,128)(4,1)S(1)} %bitcast.73, f32[2,512,8,64]{1,3,2,0:T(8,128)} %copy.40, f32[2,128,8,64]{1,0,3,2:T(2,128)S(1)} %copy-done.9), kind=kOutput, calls=%fused_computation.15 | convolution fusion | flops 808450048 | bytes 6824960 | tf_op jit(solution)/shard_map/jvp(pqhd,pkhd->phqk)/dot_general | solution.py:54
  63.2 1.3 fusion.45
  64.5 4.4 %fusion.14 = f32[2,512,8,64]{1,3,2,0:T(8,128)} fusion(f32[2,8,128]{2,1,0:T(8,128)S(1)} %fusion.45, f32[2,8,64,128]{3,0,2,1:T(2,128)S(1)} %bitcast.71, f32[2,8,128,512]{3,2,1,0:T(8,128)S(1)} %get-tuple-element.25, f32[2,8,128]{2,1,0:T(8,128)S(1)} %get-tuple-element.24, pred[2,512]{1,0:T(4,128)(4,1)S(1)} %bitcast.75), kind=kOutput, calls=%fused_computation.30 | convolution fusion | flops 809500672 | bytes 6833152 | tf_op jit(solution)/shard_map/transpose(jvp(phqk,pkhd->pqhd))/dot_general | solution.py:62
  69.0 5.6 %convert_reduce_fusion = (f32[2,8,128]{2,1,0:T(8,128)S(1)}, pred[2,8,128,512]{3,2,1,0:T(32,128)(4,1)S(1)}, f32[2,8,128]{2,1,0:T(8,128)S(1)}, f32[2,8,128,512]{3,2,1,0:T(8,128)S(1)}) fusion(f32[2,8,128]{2,1,0:T(8,128)S(1)} %get-tuple-element.24, f32[2,8,128,512]{3,2,1,0:T(8,128)S(1)} %get-tuple-element.25, pred[2,512]{1,0:T(4,128)(4,1)S(1)} %bitcast.76, ...), kind=kOutput, calls=%fused_computation.5 | convolution fusion | flops 814739456 | bytes 12092416 | tf_op jit(solution)/shard_map/transpose(jvp(phqk,pkhd->pqhd))/dot_general | solution.py:62
  74.6 2.2 fusion.59
  76.8 1.9 copy-done.2
  78.8 4.6 %fusion.15 = f32[2,512,8,64]{1,3,2,0:T(8,128)} fusion(f32[2,8,128,512]{3,2,1,0:T(8,128)S(1)} %get-tuple-element.16, pred[2,8,128,512]{3,2,1,0:T(32,128)(4,1)S(1)} %get-tuple-element.18, f32[2,8,128]{2,1,0:T(8,128)S(1)} %negate_divide_fusion, pred[2,512]{1,0:T(4,128)(4,1)S(1)} %bitcast.78, f32[2,128,8,64]{1,0,3,2:T(2,128)S(1)} %copy-done.9), kind=kOutput, calls=%fused_computation.31 | convolution fusion | flops 809500672 | bytes 7873536 | tf_op jit(solution)/shard_map/transpose(jvp(pqhd,pkhd->phqk))/dot_general | solution.py:54
  83.4 3.8 copy.56
  87.2 4.8 %reshape.224 = f32[8,128,512]{2,1,0:T(8,128)} reshape(f32[2,512,8,64]{3,2,1,0:T(8,128)} %copy.56) | data formatting | bytes 4194304 | tf_op jit(solution)/shard_map/transpose(jvp())/reshape | solution.py:47
  92.0 3.8 copy.57
  95.9 4.8 %reshape.225 = f32[8,128,512]{2,1,0:T(8,128)} reshape(f32[2,512,8,64]{3,2,1,0:T(8,128)} %copy.57) | data formatting | bytes 4194304 | tf_op jit(solution)/shard_map/transpose(jvp())/reshape | solution.py:50
  100.7 1.4 broadcast.104.clone
  102.1 5.0 %scatter_fusion = f32[6,128,512]{2,1,0:T(8,128)} fusion(f32[6,128,512]{2,1,0:T(8,128)} %broadcast.104.clone, s32[8]{0:T(128)S(1)} %reshape.186, f32[8,128,512]{2,1,0:T(8,128)} %reshape.224), kind=kCustom, calls=%fused_computation.2 | custom fusion | flops 524288 | bytes 6291488 | tf_op jit(solution)/shard_map/transpose(jvp())/scatter-add | solution.py:47
  107.3 3.4 scatter_fusion.1
  110.7 1.5 fusion.18
  112.2 1.8 collective-permute-start.3
  114.0 9.1 %collective-permute-start.2 = (f32[256,1024]{1,0:T(8,128)S(1)}, f32[256,1024]{1,0:T(8,128)S(1)}, u32[]{:S(2)}, u32[]{:S(2)}) collective-permute-start(f32[256,1024]{1,0:T(8,128)S(1)} %get-tuple-element.20), channel_id=1, source_target_pairs={{0,252},{4,0},{8,4},{12,8},{16,12},{20,16},{24,20},{28,24},{32,28}... | collective-permute-start | bytes 3145736 | tf_op jit(solution)/shard_map/ppermute | solution.py:29
  123.1 6.9 %fusion.16 = f32[2,128,8,64]{1,3,2,0:T(8,128)S(1)} fusion(f32[2,512,8,64]{1,3,2,0:T(8,128)} %copy.41, f32[2,8,128]{2,1,0:T(8,128)S(1)} %fusion.45, f32[2,8,128,512]{3,2,1,0:T(8,128)S(1)} %copy-done.5, f32[2,8,128]{2,1,0:T(8,128)S(1)} %get-tuple-element.24, pred[2,512]{1,0:T(4,128)(4,1)S(1)} %bitcast.79), kind=kOutput, calls=%fused_computation.32 | convolution fusion | flops 809500672 | bytes 6833152 | tf_op jit(solution)/shard_map/jvp(phqk,pkhd->pqhd)/dot_general | solution.py:62
  130.5 5.6 %fusion.17 = f32[2,128,8,64]{1,3,2,0:T(8,128)S(1)} fusion(f32[2,512,8,64]{1,3,2,0:T(8,128)S(1)} %copy-done.6, f32[2,8,128,512]{3,2,1,0:T(8,128)S(1)} %copy-done.3, pred[2,8,128,512]{3,2,1,0:T(32,128)(4,1)S(1)} %copy-done.17, f32[2,8,128]{2,1,0:T(8,128)S(1)} %negate_divide_fusion, pred[2,512]{1,0:T(4,128)(4,1)S(1)} %bitcast.80), kind=kOutput, calls=%fused_computation.36 | convolution fusion | flops 809500672 | bytes 7873536 | tf_op jit(solution)/shard_map/transpose(jvp(pqhd,pkhd->phqk))/dot_general | solution.py:54
  136.5 2.0 fusion.26
  138.5 2.9 fusion.22
  141.4 1.3 fusion.21
  142.7 2.1 fusion.36
  144.9 2.1 fusion.33
  147.0 3.6 fusion.24
  150.7 3.1 convolution_add_fusion.2
  154.8 1.9 multiply_reduce_fusion.1
  156.7 78.4 %psum.35 = f32[512]{0:T(512)} all-reduce(f32[512]{0:T(512)S(1)} %get-tuple-element.7), channel_id=1, replica_groups=mesh['space'=64,'slab'=4] {'space','slab'}, use_global_device_ids=true, to_apply=%region_12.13 | all-reduce | flops 512 | bytes 4096 | tf_op jit(solution)/shard_map/psum | solution.py:121
  235.1 1.3 fusion.58
  237.3 176.7 %all-reduce.4.cloned.1.call-done = (f32[512,512]{1,0:T(8,128)}, f32[512,512]{1,0:T(8,128)}, f32[512,512]{1,0:T(8,128)}, f32[512,512]{1,0:T(8,128)}) async-done(((f32[512,512]{1,0:T(8,128)}, f32[512,512]{1,0:T(8,128)}, f32[512,512]{1,0:T(8,128)}, f32[512,512]{1,0:T(8,128)}), (f32[512,512]{1,0:T(8,128)}, f32[512,512]{1,0:T(8,128)}, f32[512,512]{1,0:T(8,128)}, ...) | async-done | bytes 4194320 | tf_op jit(solution)/shard_map/psum | solution.py:121
  414.0 2.4 copy.107
  416.4 2.3 copy.108
  (83 shorter events, 9.1 us)
Async XLA Ops:
  7.2 2.6 copy-start
  7.2 12.2 %copy-start.1 = (f32[256,512]{1,0:T(8,128)S(1)}, f32[256,512]{1,0:T(8,128)}, u32[]{:S(2)}) copy-start(f32[256,512]{1,0:T(8,128)} %param.9) | copy-start | bytes 1572868
  7.2 12.2 %copy-start.23 = (f32[512]{0:T(512)S(1)}, f32[512]{0:T(512)}, u32[]{:S(2)}) copy-start(f32[512]{0:T(512)} %param.10) | copy-start | bytes 6148
  7.2 11.8 %copy-start.24 = (s32[2,3]{1,0:T(2,128)S(1)}, s32[2,3]{1,0:T(2,128)}, u32[]{:S(2)}) copy-start(s32[2,3]{1,0:T(2,128)} %param.15) | copy-start | bytes 76
  7.2 11.9 %copy-start.25 = (s32[2]{0:T(128)S(1)}, s32[2]{0:T(128)}, u32[]{:S(2)}) copy-start(s32[2]{0:T(128)} %param.16) | copy-start | bytes 28
  7.2 406.8 %all-reduce.4.cloned.1.call-start = ((), (), s32[]{:S(2)}) async-start(), calls=%async_computation | async-start | bytes 8388608 | tf_op jit(solution)/shard_map/psum | solution.py:121
  12.0 13.4 %copy-start.13 = (f32[256,512]{1,0:T(8,128)S(1)}, f32[256,512]{1,0:T(8,128)}, u32[]{:S(2)}) copy-start(f32[256,512]{1,0:T(8,128)} %param.17) | copy-start | bytes 1572868
  15.6 16.1 %collective-permute-start.1 = (f32[256,1024]{1,0:T(8,128)}, f32[256,1024]{1,0:T(8,128)}, u32[]{:S(2)}, u32[]{:S(2)}) collective-permute-start(f32[256,1024]{1,0:T(8,128)} %pad_maximum_fusion.2), channel_id=1, source_target_pairs={{4,0},{8,4},{12,8},{16,12},{20,16},{24,20},{28,24},{32,28},{36,32}... | collective-permute-start | bytes 3145736 | tf_op jit(solution)/shard_map/ppermute | solution.py:19
  18.9 12.9 %collective-permute-start = (f32[256,1024]{1,0:T(8,128)}, f32[256,1024]{1,0:T(8,128)}, u32[]{:S(2)}, u32[]{:S(2)}) collective-permute-start(f32[256,1024]{1,0:T(8,128)} %pad_maximum_fusion.2), channel_id=1, source_target_pairs={{0,4},{4,8},{8,12},{12,16},{16,20},{20,24},{24,28},{28,32},{32,36}... | collective-permute-start | bytes 3145736 | tf_op jit(solution)/shard_map/ppermute | solution.py:17
  53.6 3.9 copy-start.9
  57.5 7.1 %copy-start.22 = (f32[2,128,8,64]{1,0,3,2:T(2,128)S(1)}, f32[2,128,8,64]{1,0,3,2:T(2,128)}, u32[]{:S(2)}) copy-start(f32[2,128,8,64]{1,0,3,2:T(2,128)} %reshape.178) | copy-start | bytes 1572868
  63.2 11.5 %copy-start.4 = (f32[2,8,128,512]{3,2,1,0:T(8,128)}, f32[2,8,128,512]{3,2,1,0:T(8,128)S(1)}, u32[]{:S(2)}) copy-start(f32[2,8,128,512]{3,2,1,0:T(8,128)S(1)} %get-tuple-element.25) | copy-start | bytes 12582916
  64.5 4.5 %copy-start.19 = (f32[2,512,8,64]{1,3,2,0:T(8,128)S(1)}, f32[2,512,8,64]{1,3,2,0:T(8,128)}, u32[]{:S(2)}) copy-start(f32[2,512,8,64]{1,3,2,0:T(8,128)} %copy.41) | copy-start | bytes 6291460
  74.6 2.2 copy-start.16
  76.8 2.0 copy-start.2
  110.7 12.4 %copy-start.5 = (f32[2,8,128,512]{3,2,1,0:T(8,128)S(1)}, f32[2,8,128,512]{3,2,1,0:T(8,128)}, u32[]{:S(2)}) copy-start(f32[2,8,128,512]{3,2,1,0:T(8,128)} %copy-done.4) | copy-start | bytes 12582916
  112.2 29.2 %collective-permute-start.3 = (f32[256,1024]{1,0:T(8,128)S(1)}, f32[256,1024]{1,0:T(8,128)S(1)}, u32[]{:S(2)}, u32[]{:S(2)}) collective-permute-start(f32[256,1024]{1,0:T(8,128)S(1)} %get-tuple-element.21), channel_id=1, source_target_pairs={{0,4},{4,8},{8,12},{12,16},{16,20},{20,24},{24,28},{28,32},{32,36}... | collective-permute-start | bytes 3145736 | tf_op jit(solution)/shard_map/ppermute | solution.py:29
  114.0 16.4 %copy-start.3 = (f32[2,8,128,512]{3,2,1,0:T(8,128)S(1)}, f32[2,8,128,512]{3,2,1,0:T(8,128)}, u32[]{:S(2)}) copy-start(f32[2,8,128,512]{3,2,1,0:T(8,128)} %copy-done.2) | copy-start | bytes 12582916
  114.0 16.4 %copy-start.6 = (f32[2,512,8,64]{1,3,2,0:T(8,128)S(1)}, f32[2,512,8,64]{1,3,2,0:T(8,128)}, u32[]{:S(2)}) copy-start(f32[2,512,8,64]{1,3,2,0:T(8,128)} %copy.40) | copy-start | bytes 6291460
  114.0 16.5 %copy-start.17 = (pred[2,8,128,512]{3,2,1,0:T(32,128)(4,1)S(1)}, pred[2,8,128,512]{3,2,1,0:T(32,128)(4,1)}, u32[]{:S(2)}) copy-start(pred[2,8,128,512]{3,2,1,0:T(32,128)(4,1)} %copy-done.16) | copy-start | bytes 3145732
  114.0 27.4 %collective-permute-start.2 = (f32[256,1024]{1,0:T(8,128)S(1)}, f32[256,1024]{1,0:T(8,128)S(1)}, u32[]{:S(2)}, u32[]{:S(2)}) collective-permute-start(f32[256,1024]{1,0:T(8,128)S(1)} %get-tuple-element.20), channel_id=1, source_target_pairs={{0,252},{4,0},{8,4},{12,8},{16,12},{20,16},{24,20},{28,24},{32,28}... | collective-permute-start | bytes 3145736 | tf_op jit(solution)/shard_map/ppermute | solution.py:29
  130.4 6.0 %copy-start.10 = (f32[2,128,8,64]{1,0,3,2:T(2,128)}, f32[2,128,8,64]{1,0,3,2:T(2,128)S(1)}, u32[]{:S(2)}) copy-start(f32[2,128,8,64]{1,0,3,2:T(2,128)S(1)} %copy.42) | copy-start | bytes 1572868
  130.4 6.0 %copy-start.14 = (f32[256,512]{1,0:T(8,128)S(1)}, f32[256,512]{1,0:T(8,128)}, u32[]{:S(2)}) copy-start(f32[256,512]{1,0:T(8,128)} %param.17) | copy-start | bytes 1572868
  136.5 5.0 %copy-start.12 = (f32[2,128,8,64]{1,0,3,2:T(2,128)}, f32[2,128,8,64]{1,0,3,2:T(2,128)S(1)}, u32[]{:S(2)}) copy-start(f32[2,128,8,64]{1,0,3,2:T(2,128)S(1)} %copy.47) | copy-start | bytes 1572868
  142.7 2.1 copy-start.7
  144.9 5.8 %copy-start.11 = (f32[2,128,8,64]{1,0,3,2:T(2,128)S(1)}, f32[2,128,8,64]{1,0,3,2:T(2,128)}, u32[]{:S(2)}) copy-start(f32[2,128,8,64]{1,0,3,2:T(2,128)} %copy-done.10) | copy-start | bytes 1572868
  147.0 6.8 %copy-start.8 = (f32[256,1024]{1,0:T(8,128)S(1)}, f32[256,1024]{1,0:T(8,128)}, u32[]{:S(2)}) copy-start(f32[256,1024]{1,0:T(8,128)} %copy-done.7) | copy-start | bytes 3145732
  147.0 6.7 %copy-start.18 = (f32[512,512]{1,0:T(8,128)S(1)}, f32[512,512]{1,0:T(8,128)}, u32[]{:S(2)}) copy-start(f32[512,512]{1,0:T(8,128)} %param.12) | copy-start | bytes 3145732
  153.8 82.7 %copy-start.15 = (f32[256,512]{1,0:T(8,128)S(1)}, f32[256,512]{1,0:T(8,128)}, u32[]{:S(2)}) copy-start(f32[256,512]{1,0:T(8,128)} %param.17) | copy-start | bytes 1572868
  414.0 4.7 %copy-start.21 = (f32[512,512]{1,0:T(8,128)S(1)}, f32[512,512]{1,0:T(8,128)}, u32[]{:S(2)}) copy-start(f32[512,512]{1,0:T(8,128)} %get-tuple-element.33) | copy-start | bytes 3145732
  414.0 5.7 %copy-start.20 = (f32[512,512]{1,0:T(8,128)S(1)}, f32[512,512]{1,0:T(8,128)}, u32[]{:S(2)}) copy-start(f32[512,512]{1,0:T(8,128)} %get-tuple-element.34) | copy-start | bytes 3145732
Sparse Core Ops, SparseCore 0:
  147.1 266.8 all-reduce.3
where the time goes:
time: 436 us; the launch traced here: 428 us
  waiting for transfers between devices  178 us (41%)
  blocking collectives  78.4 us (18%)
  matrix products  63.4 us (15%)
  local copies, waits for them, and re-layouts  56.7 us (13%)
  other arithmetic  22.6 us (5%)
  between operations  14.9 us (3%)
  starting transfers between devices  14.1 us (3%)
    psum x1, waiting for transfers between devices, body(): lax.psum((grad_gain, grad_query, grad_key, grad_value, grad_output), ('sp...  177 us
    psum x1, blocking collectives, body(): lax.psum((grad_gain, grad_query, grad_key, grad_value, grad_output), ('sp...  78.4 us
    dot_general x12, matrix products, matmul(): jnp.dot(left, right, precision=lax.Precision.HIGHEST, preferred_element_t...  30.5 us
    reshape x4, local copies, waits for them, and re-layouts, attention(): value_win.reshape(-1, PT, model_width)[block_index]  17.3 us
    dot_general x3, matrix products, attention(): jnp.einsum('phqk,pkhd->pqhd', probability, picked_values, precision=lax.P...  17 us
    reshape x4, local copies, waits for them, and re-layouts, attention(): key_win.reshape(-1, PT, model_width)[block_index]  16.9 us
    dot_general x3, matrix products, attention(): jnp.einsum('pqhd,pkhd->phqk', query_blocks, picked_keys, precision=lax.Pr...  15.9 us
    ppermute x2, starting transfers between devices, passed_along(): return lax.ppermute(value, axis, pairs)  10.8 us
  transfers between devices with their start and end apart: 5, of which 2 were waited for; matrix products, arithmetic and copies ran while one was open for 10% of the time, Pallas kernels for 0%

commit v1 on v0

v1 whole, which is shorter than its diff:
```python
import jax
import jax.numpy as jnp
from jax import lax
from jax.experimental import pallas as pl
from jax.experimental.pallas import tpu as pltpu
from jax.sharding import PartitionSpec as P

MESH = pl.DeviceIdType.MESH
F32 = jnp.float32
BF16 = jnp.bfloat16
HEADS = 8
PT = 128
D = 512
HD = D // HEADS
ROWS = 256
WIN = 3 * ROWS
NX, NY, NZ = 4, 4, 8

NN = (((1,), (0,)), ((), ()))
NT = (((1,), (1,)), ((), ()))


def coords():
    s = lax.axis_index("space")
    y = lax.axis_index("slab")
    return s, s // (2 * NZ), y, (s // 2) % NZ, s % 2


def device(x, y, z, core):
    return {"space": (x * NZ + z) * 2 + core, "slab": y}


def halo_kernel(tok, left, right, send, recv):
    s = lax.axis_index("space")
    count = lax.axis_size("space")
    after = {"space": (s + 1) % count}
    before = {"space": (s + count - 1) % count}
    barrier = pltpu.get_barrier_semaphore()
    for peer in (after, before):
        pl.semaphore_signal(barrier, inc=1, device_id=peer, device_id_type=MESH)
    pl.semaphore_wait(barrier, 2)
    to_after = pltpu.make_async_remote_copy(tok, left, send.at[0], recv.at[0], device_id=after, device_id_type=MESH)
    to_before = pltpu.make_async_remote_copy(tok, right, send.at[1], recv.at[1], device_id=before, device_id_type=MESH)
    to_after.start()
    to_before.start()
    to_after.wait()
    to_before.wait()


def halo(tokens):
    shape = jax.ShapeDtypeStruct(tokens.shape, F32)
    hbm = pl.BlockSpec(memory_space=pl.ANY)
    return pl.pallas_call(
        halo_kernel,
        out_shape=(shape, shape),
        in_specs=[hbm],
        out_specs=(hbm, hbm),
        scratch_shapes=[pltpu.SemaphoreType.DMA((2,)), pltpu.SemaphoreType.DMA((2,))],
        compiler_params=pltpu.CompilerParams(collective_id=0, has_side_effects=True),
        name="halo",
    )(tokens)


def split(value):
    high = value.astype(BF16)
    return high, (value - high.astype(F32)).astype(BF16)


def dot(left, right, dims):
    return lax.dot_general(left, right, dims, preferred_element_type=F32)


def dot3(left, right, dims=NN):
    lh, ll = left
    rh, rl = right
    return dot(lh, rh, dims) + (dot(lh, rl, dims) + dot(ll, rh, dims))


def pair(ref, *index):
    return ref[(0,) + index], ref[(1,) + index]


def put(ref, value, *index):
    high, low = split(value)
    ref[(0,) + index] = high
    ref[(1,) + index] = low


ALL = slice(None)


def layer_kernel(
    nlist, ncount, tok, left, right, gain, wq, wk, wv, wo, cot,
    result, grads, dgain, dtok, dhalo,
    xhat, rstd, hid_t, k2, v2, kt2, vt2, q2, do2, do_t, o_t, dq_t, dk, dv, w2, bias,
):
    gain_row = gain[...]
    for i, ref in enumerate((left, tok, right)):
        rows = slice(i * ROWS, (i + 1) * ROWS)
        x = ref[...]
        centred = x - jnp.mean(x, axis=1, keepdims=True)
        inv = lax.rsqrt(jnp.mean(centred * centred, axis=1, keepdims=True) + 1e-5)
        xhat[rows] = centred * inv
        rstd[rows] = inv
    for i, ref in enumerate((wq, wk, wv, wo)):
        put(w2.at[i], ref[...])
    for w in range(6):
        for p in range(2):
            if w == 2 + p:
                flag = 0.0
            else:
                flag = -1e30
                for j in range(3):
                    live = jnp.logical_and(nlist[p, j] == w, j < ncount[p])
                    flag = jnp.where(live, 0.0, flag)
            bias[w * PT : (w + 1) * PT, p * PT : (p + 1) * PT] = jnp.full((PT, PT), flag, F32)
    hidden = xhat[...] * gain_row
    put(hid_t, hidden.T, ALL, ALL)
    hid2 = split(hidden)
    own2 = (hid2[0][ROWS : 2 * ROWS], hid2[1][ROWS : 2 * ROWS])
    put(q2, dot3(own2, pair(w2.at[0], ALL, ALL)), ALL, ALL)
    keys = dot3(hid2, pair(w2.at[1], ALL, ALL))
    put(k2, keys, ALL, ALL)
    put(kt2, keys.T, ALL, ALL)
    values = dot3(hid2, pair(w2.at[2], ALL, ALL))
    put(v2, values, ALL, ALL)
    put(vt2, values.T, ALL, ALL)
    cot2 = split(cot[...])
    d_mixed = dot3(cot2, pair(w2.at[3], ALL, ALL), NT)
    put(do2, d_mixed, ALL, ALL)
    do_t[...] = d_mixed.T

    @pl.loop(0, HEADS // 2)
    def _(hp):
        lanes = pl.ds(pl.multiple_of(hp * 2 * HD, 2 * HD), 2 * HD)
        q_pair, k_pair, v_pair, do_pair = (pair(ref, ALL, lanes) for ref in (q2, k2, v2, do2))
        dks, dvs = [], []
        for half in range(2):
            sl = slice(half * HD, (half + 1) * HD)
            q_h, k_h, v_h, do_h = ((a[:, sl], b[:, sl]) for a, b in (q_pair, k_pair, v_pair, do_pair))
            feats = pl.ds(pl.multiple_of(hp * 2 * HD + half * HD, HD), HD)
            scores = dot3(k_h, q_h, NT) * HD**-0.5 + bias[...]
            weights = jnp.exp(scores - jnp.max(scores, axis=0, keepdims=True))
            prob = weights * (1.0 / jnp.sum(weights, axis=0, keepdims=True))
            prob2 = split(prob)
            mixed_t = dot3(pair(vt2, feats, ALL), prob2)
            o_t[feats] = mixed_t
            dvs.append(dot3(prob2, do_h))
            d_prob = dot3(v_h, do_h, NT)
            inner = jnp.sum(mixed_t * do_t[feats], axis=0, keepdims=True)
            d_scores2 = split(prob * (d_prob - inner) * HD**-0.5)
            dq_t[feats] = dot3(pair(kt2, feats, ALL), d_scores2)
            dks.append(dot3(d_scores2, q_h))
        dk[:, lanes] = jnp.concatenate(dks, axis=1)
        dv[:, lanes] = jnp.concatenate(dvs, axis=1)

    mixed_t = o_t[...]
    grads[3] = dot3(split(mixed_t), cot2)
    result[...] = dot3(split(mixed_t.T), pair(w2.at[3], ALL, ALL)) + tok[...]
    dq_all = dq_t[...]
    own_t = pair(hid_t, ALL, slice(ROWS, 2 * ROWS))
    grads[0] = dot3(own_t, split(dq_all), NT)
    dk2 = split(dk[...])
    grads[1] = dot3(pair(hid_t, ALL, ALL), dk2)
    dv2 = split(dv[...])
    grads[2] = dot3(pair(hid_t, ALL, ALL), dv2)
    d_hidden = dot3(dk2, pair(w2.at[1], ALL, ALL), NT) + dot3(dv2, pair(w2.at[2], ALL, ALL), NT)
    dq_part = dot3(split(dq_all.T), pair(w2.at[0], ALL, ALL), NT)
    total = jnp.zeros((1, D), F32)
    for i in range(3):
        rows = slice(i * ROWS, (i + 1) * ROWS)
        part = d_hidden[rows]
        if i == 1:
            part = part + dq_part
        hat = xhat[rows]
        weighted = part * hat
        total = total + jnp.sum(weighted, axis=0, keepdims=True)
        grad = part * gain_row
        inner = jnp.mean(weighted * gain_row, axis=1, keepdims=True)
        grad = rstd[rows] * (grad - jnp.mean(grad, axis=1, keepdims=True) - hat * inner)
        if i == 1:
            dtok[...] = grad + cot[...]
        else:
            dhalo[i // 2] = grad
    dgain[...] = jnp.broadcast_to(total, dgain.shape)


def layer(nlist, ncount, tokens, left, right, gain, wq, wk, wv, wo, cot):
    vmem = pl.BlockSpec(memory_space=pltpu.VMEM)
    smem = pl.BlockSpec(memory_space=pltpu.SMEM)
    shape = jax.ShapeDtypeStruct
    return pl.pallas_call(
        layer_kernel,
        out_shape=(
            shape((ROWS, D), F32),
            shape((4, D, D), F32),
            shape((8, D), F32),
            shape((ROWS, D), F32),
            shape((2, ROWS, D), F32),
        ),
        in_specs=[smem] * 2 + [vmem] * 9,
        out_specs=(vmem,) * 5,
        scratch_shapes=[
            pltpu.VMEM((WIN, D), F32),
            pltpu.VMEM((WIN, 1), F32),
            pltpu.VMEM((2, D, WIN), BF16),
            pltpu.VMEM((2, WIN, D), BF16),
            pltpu.VMEM((2, WIN, D), BF16),
            pltpu.VMEM((2, D, WIN), BF16),
            pltpu.VMEM((2, D, WIN), BF16),
            pltpu.VMEM((2, ROWS, D), BF16),
            pltpu.VMEM((2, ROWS, D), BF16),
            pltpu.VMEM((D, ROWS), F32),
            pltpu.VMEM((D, ROWS), F32),
            pltpu.VMEM((D, ROWS), F32),
            pltpu.VMEM((WIN, D), F32),
            pltpu.VMEM((WIN, D), F32),
            pltpu.VMEM((4, 2, D, D), BF16),
            pltpu.VMEM((WIN, ROWS), F32),
        ],
        compiler_params=pltpu.CompilerParams(vmem_limit_bytes=58 << 20),
        name="layer",
    )(nlist, ncount, tokens, left, right, gain, wq, wk, wv, wo, cot)


def sum_kernel(
    grads, gain_part, dtok, dhalo,
    out, dgain, dtokens,
    own, r0, r1, acc2, r2, acc3, r3, g0, g1, g2, g3, gs, halo_in,
    send0, recv0, send1, recv1, send2, recv2, send3, recv3, send4, recv4, send5, recv5, send6, recv6, send7, recv7,
    gsend, grecv, hsend, hrecv,
):
    s, x, y, z, c = coords()
    count = lax.axis_size("space")
    partner = device(x, y, z, 1 - c)
    xs = [(x + d) % NX for d in range(NX)]
    ys = [(y + d) % NY for d in range(NY)]
    zs = [(z + d) % NZ for d in range(NZ)]
    x_peers = [device(i, y, z, c) for i in xs]
    y_peers = [device(x, i, z, c) for i in ys]
    z_peers = [device(x, y, i, c) for i in zs]
    after = {"space": (s + 1) % count, "slab": y}
    before = {"space": (s + count - 1) % count, "slab": y}
    other = {"space": (s + count - 1 + 2 * c) % count, "slab": y}
    barrier = pltpu.get_barrier_semaphore()
    everyone = [partner, other] + x_peers[1:] + y_peers[1:] + z_peers[1:]
    for peer in everyone:
        pl.semaphore_signal(barrier, inc=1, device_id=peer, device_id_type=MESH)
    pl.semaphore_wait(barrier, len(everyone))

    sent = []

    def send(src, dst, send_sem, recv_sem, peer):
        copy = pltpu.make_async_remote_copy(src, dst, send_sem, recv_sem, device_id=peer, device_id_type=MESH)
        copy.start()
        sent.append(copy)
        return copy

    orders = []
    for m in range(4):
        orders.append(((xs, x_peers), (ys, y_peers)) if m % 2 == 0 else ((ys, y_peers), (xs, x_peers)))
    mine = pl.ds(pl.multiple_of(c * 256, 128), 256)
    theirs = pl.ds(pl.multiple_of((1 - c) * 256, 128), 256)

    first = [send(grads.at[m, :, theirs], r0.at[m], send0.at[m], recv0.at[m], partner) for m in range(4)]
    gain_copies = [send(gain_part, g0, gsend.at[0], grecv.at[0], partner)]
    halo_copies = [
        send(dhalo.at[0], halo_in.at[1], hsend.at[0], hrecv.at[0], before),
        send(dhalo.at[1], halo_in.at[0], hsend.at[1], hrecv.at[1], after),
    ]
    second = []
    for m in range(4):
        first[m].wait_recv()
        own[m] = grads[m, :, mine] + r0[m]
        index, peers = orders[m][0]
        second.append(
            [
                send(
                    own.at[m, pl.ds(pl.multiple_of(index[d] * 128, 128), 128)],
                    r1.at[m, d - 1],
                    send1.at[m, d - 1],
                    recv1.at[m, d - 1],
                    peers[d],
                )
                for d in range(1, 4)
            ]
        )
    gain_copies[0].wait_recv()
    gs[0, c] = gain_part[...]
    gs[0, 1 - c] = g0[...]
    value = gs[0, 0] + gs[0, 1]
    for level, (size, peers, at, landing) in enumerate(((NX, x_peers, x, g1), (NY, y_peers, y, g2), (NZ, z_peers, z, g3))):
        gs[level + 1, at] = value
        base = (1, 4, 7)[level]
        copies = [
            send(gs.at[level + 1, at], landing.at[d - 1], gsend.at[base + d - 1], grecv.at[base + d - 1], peers[d])
            for d in range(1, size)
        ]
        for d in range(1, size):
            copies[d - 1].wait_recv()
            gs[level + 1, (at + size - d) % size] = landing[d - 1]
        value = gs[level + 1, 0]
        for i in range(1, size):
            value = value + gs[level + 1, i]
    dgain[...] = value

    third = []
    for m in range(4):
        for copy in second[m]:
            copy.wait_recv()
        at = pl.ds(pl.multiple_of(orders[m][0][0][0] * 128, 128), 128)
        acc2[m] = own[m, at] + r1[m, 0] + r1[m, 1] + r1[m, 2]
        index, peers = orders[m][1]
        third.append(
            [
                send(
                    acc2.at[m, pl.ds(pl.multiple_of(index[d] * 32, 32), 32)],
                    r2.at[m, d - 1],
                    send2.at[m, d - 1],
                    recv2.at[m, d - 1],
                    peers[d],
                )
                for d in range(1, 4)
            ]
        )

    def tile(i):
        return pl.ds(pl.multiple_of((i % 4) * 8, 8), 8), pl.ds(pl.multiple_of((i // 4) * 128, 128), 128)

    fourth = []
    for m in range(4):
        for copy in third[m]:
            copy.wait_recv()
        at = pl.ds(pl.multiple_of(orders[m][1][0][0] * 32, 32), 32)
        acc3[m] = acc2[m, at] + r2[m, 0] + r2[m, 1] + r2[m, 2]
        fourth.append(
            [
                send(acc3.at[(m,) + tile(zs[d])], r3.at[m, d - 1], send3.at[m, d - 1], recv3.at[m, d - 1], z_peers[d])
                for d in range(1, 8)
            ]
        )
    for copy in halo_copies:
        copy.wait_recv()
    dtokens[...] = dtok[...] + halo_in[0] + halo_in[1]

    def place(m, level):
        a1, a2 = orders[m][0][0][0], orders[m][1][0][0]
        if level == 0:
            return m, pl.ds(0, D), mine
        if level == 1:
            return m, pl.ds(pl.multiple_of(a1 * 128, 128), 128), mine
        row = a1 * 128 + a2 * 32
        if level == 2:
            return m, pl.ds(pl.multiple_of(row, 32), 32), mine
        return (
            m,
            pl.ds(pl.multiple_of(row + (z % 4) * 8, 8), 8),
            pl.ds(pl.multiple_of(c * 256 + (z // 4) * 128, 128), 128),
        )

    fifth = []
    for m in range(4):
        for copy in fourth[m]:
            copy.wait_recv()
        total = acc3[(m,) + tile(z)]
        for d in range(7):
            total = total + r3[m, d]
        block = place(m, 3)
        out[block] = total
        fifth.append(
            [send(out.at[block], out.at[block], send4.at[m, d - 1], recv4.at[m, d - 1], z_peers[d]) for d in range(1, 8)]
        )
    latest = fifth
    for level, (ss, rs) in enumerate(((send5, recv5), (send6, recv6), (send7, recv7))):
        copies, latest = latest, []
        for m in range(4):
            for copy in copies[m]:
                copy.wait_recv()
            block = place(m, 2 - level)
            peers = ([partner], orders[m][0][1][1:], orders[m][1][1][1:])[2 - level]
            latest.append(
                [send(out.at[block], out.at[block], ss.at[m, i], rs.at[m, i], peer) for i, peer in enumerate(peers)]
            )
    for m in range(4):
        for copy in latest[m]:
            copy.wait_recv()
    for copy in sent:
        copy.wait_send()


def sum_all(grads, gain_part, dtok, dhalo):
    vmem = pl.BlockSpec(memory_space=pltpu.VMEM)
    shape = jax.ShapeDtypeStruct
    dma = pltpu.SemaphoreType.DMA
    sems = []
    for peers in (1, 3, 3, 7, 7, 3, 3, 1):
        kind = dma((4,)) if peers == 1 and not sems else dma((4, peers))
        sems += [kind, kind]
    return pl.pallas_call(
        sum_kernel,
        out_shape=(shape((4, D, D), F32), shape((8, D), F32), shape((ROWS, D), F32)),
        in_specs=[vmem] * 4,
        out_specs=(vmem,) * 3,
        scratch_shapes=[
            pltpu.VMEM((4, D, 256), F32),
            pltpu.VMEM((4, D, 256), F32),
            pltpu.VMEM((4, 3, 128, 256), F32),
            pltpu.VMEM((4, 128, 256), F32),
            pltpu.VMEM((4, 3, 32, 256), F32),
            pltpu.VMEM((4, 32, 256), F32),
            pltpu.VMEM((4, 7, 8, 128), F32),
            pltpu.VMEM((8, D), F32),
            pltpu.VMEM((3, 8, D), F32),
            pltpu.VMEM((3, 8, D), F32),
            pltpu.VMEM((7, 8, D), F32),
            pltpu.VMEM((4, 8, 8, D), F32),
            pltpu.VMEM((2, ROWS, D), F32),
        ]
        + sems
        + [dma((14,)), dma((14,)), dma((2,)), dma((2,))],
        compiler_params=pltpu.CompilerParams(
            collective_id=1, has_side_effects=True, vmem_limit_bytes=48 << 20
        ),
        name="sum_all",
    )(grads, gain_part, dtok, dhalo)


def body(tokens, gain, wq, wk, wv, wo, nlist, ncount, cot):
    left, right = halo(tokens)
    result, grads, gain_part, dtok, dhalo = layer(
        nlist, ncount, tokens, left, right, gain[None, :], wq, wk, wv, wo, cot
    )
    sums, gain_sum, d_tokens = sum_all(grads, gain_part, dtok, dhalo)
    return (result, d_tokens, gain_sum[0], sums[0], sums[1], sums[2], sums[3])


def solution(mesh):
    rows = P(("space", "slab"), None)
    return jax.shard_map(
        body,
        mesh=mesh,
        in_specs=(rows, P(), P(), P(), P(), P(), rows, P(("space", "slab")), rows),
        out_specs=(rows, rows, P(), P(), P(), P(), P()),
        check_vma=False,
    )
```

time: 436 us -> 131 us (0.30); the launches traced: 428 us -> 131 us
  waiting for transfers between devices: 178 us -> 0 us
  Pallas kernels: 0 us -> 122 us
  blocking collectives: 78.4 us -> 0 us
  matrix products: 63.4 us -> 0 us
  local copies, waits for them, and re-layouts: 56.7 us -> 8.6 us
  other arithmetic: 22.6 us -> 0 us
  between operations: 14.9 us -> 0.65 us
  starting transfers between devices: 14.1 us -> 0 us
    psum x1 -> x0, waiting for transfers between devices: 177 us -> none  [body(): lax.psum((grad_gain, grad_query, grad_key, grad_value, grad_output), ('sp...]
    pallas_call x0 -> x3, Pallas kernels: none -> 122 us  [the longest x1 76 us: sum_all(): pl.pallas_call(sum_kernel, out_shape=(shape((4, D, D), F32), shape((8, D)...]
    psum x1 -> x0, blocking collectives: 78.4 us -> none  [body(): lax.psum((grad_gain, grad_query, grad_key, grad_value, grad_output), ('sp...]
    dot_general x18 -> x0, matrix products: 63.4 us -> none  [the longest x12 30.5 us: matmul(): jnp.dot(left, right, precision=lax.Precision.HIGHEST, preferred_element_t...]
    reshape x10 -> x0, local copies, waits for them, and re-layouts: 38.4 us -> none  [the longest x4 17.3 us: attention(): value_win.reshape(-1, PT, model_width)[block_index]]
    ppermute x4 -> x0, starting transfers between devices: 14.1 us -> none  [the longest x2 10.8 us: passed_along(): return lax.ppermute(value, axis, pairs)]
    scatter-add x2 -> x0, other arithmetic: 8.39 us -> none  [the longest x1 5.02 us: attention(): key_win.reshape(-1, PT, model_width)[block_index]]
    reduce_sum x5 -> x0, other arithmetic: 7.29 us -> none  [the longest x1 2.16 us: attention(): weights = jnp.exp(scores - row_max)]
  transfers between devices with their start and end apart: 5 -> 0, of which waited for: 2 -> 0; matrix products, arithmetic and copies ran while one was open for 10% -> 0% of each run, Pallas kernels for 0% -> 0%
where the time goes in v1:
time: 131 us
  Pallas kernels  122 us (93%)
  local copies, waits for them, and re-layouts  8.6 us (7%)
    pallas_call x1, Pallas kernels, sum_all(): pl.pallas_call(sum_kernel, out_shape=(shape((4, D, D), F32), shape((8, D)...  76 us
    pallas_call x1, Pallas kernels, layer(): pl.pallas_call(layer_kernel, out_shape=(shape((ROWS, D), F32), shape((4,...  34.8 us
    pallas_call x1, Pallas kernels, halo(): pl.pallas_call(halo_kernel, out_shape=(shape, shape), in_specs=[hbm], out...  10.9 us
    squeeze x1, local copies, waits for them, and re-layouts, body(): return (result, d_tokens, gain_sum[0], sums[0], sums[1], sums[2], sums[3])  4.25 us
    unnamed x7, local copies, waits for them, and re-layouts  3.77 us

profile of v1, /device:TPU:1, one launch (start us, length us, event | category | flops | bytes accessed | tf_op | source)
XLA Modules:
  0.0 131.0 jit_solution(10211703674162488281)
XLA Ops:
  0.6 10.9 %halo.1 = (f32[256,512]{1,0:T(8,128)}, f32[256,512]{1,0:T(8,128)}) custom-call(f32[256,512]{1,0:T(8,128)} %tok.3), custom_call_target="tpu_custom_call" | custom-call | tf_op jit(solution)/shard_map/halo/pallas_call | solution.py:53
  11.6 34.8 %layer.1 = (f32[256,512]{1,0:T(8,128)}, f32[4,512,512]{2,1,0:T(8,128)}, f32[8,512]{1,0:T(8,128)}, f32[256,512]{1,0:T(8,128)}, f32[2,256,512]{2,1,0:T(8,128)}) custom-call(s32[2,3]{1,0:T(2,128)} %nlist.1, s32[2]{0:T(128)} %ncount.1, f32[256,512]{1,0:T(8,128)} %tok.3, f32[256,512]{1,0:T(8,128)} %get-tuple-element.17.left, f32[256,512]{1,0:T(8,128)} %get-tuple-element.18.right, ...), custom_call_target="tpu_custom_call" | custom-call | tf_op jit(solution)/shard_map/layer/pallas_call | solution.py:192
  46.4 0.0 copy-start
  46.4 1.2 copy-done
  47.6 0.0 copy-start.1
  47.6 1.0 copy-done.1
  48.7 0.0 copy-start.2
  48.7 0.7 copy-done.2
  49.4 76.0 %sum_all.1 = (f32[4,512,512]{2,1,0:T(8,128)}, f32[8,512]{1,0:T(8,128)S(1)}, f32[256,512]{1,0:T(8,128)S(1)}) custom-call(f32[4,512,512]{2,1,0:T(8,128)} %get-tuple-element.20.grads, f32[8,512]{1,0:T(8,128)S(1)} %copy-done.2, f32[256,512]{1,0:T(8,128)S(1)} %copy-done.1, f32[2,256,512]{2,1,0:T(8,128)S(1)} %copy-done), custom_call_target="tpu_custom_call" | custom-call | tf_op jit(solution)/shard_map/sum_all/pallas_call | solution.py:399
  125.4 0.6 slice.15
  126.0 4.2 %slice_bitcast_fusion = (f32[512,512]{1,0:T(8,128)}, f32[512,512]{1,0:T(8,128)}, f32[512,512]{1,0:T(8,128)}, f32[512,512]{1,0:T(8,128)}) fusion(f32[4,512,512]{2,1,0:T(8,128)} %get-tuple-element.26), kind=kLoop, calls=%fused_computation | loop fusion | bytes 8388608 | tf_op jit(solution)/shard_map/squeeze | solution.py:434
  130.2 0.8 copy.17
Async XLA Ops:
  46.4 1.2 copy-start
  47.6 1.0 copy-start.1
  48.7 0.7 copy-start.2

commit v2 on v0

v2 whole, which is shorter than its diff:
```python
import jax
import jax.numpy as jnp
from jax import lax
from jax.experimental import pallas as pl
from jax.experimental.pallas import tpu as pltpu
from jax.sharding import PartitionSpec as P

MESH = pl.DeviceIdType.MESH
F32 = jnp.float32
BF16 = jnp.bfloat16
HEADS = 8
PT = 128
D = 512
HD = D // HEADS
ROWS = 256
WIN = 3 * ROWS
NX, NY, NZ = 4, 4, 8
QUARTERS = 4
LANES = 128

NN = (((1,), (0,)), ((), ()))
NT = (((1,), (1,)), ((), ()))


def device(x, y, z, core):
    return {"space": (x * NZ + z) * 2 + core, "slab": y}


def split(value):
    high = value.astype(BF16)
    return high, (value - high.astype(F32)).astype(BF16)


def dot(left, right, dims=NN):
    return lax.dot_general(left, right, dims, preferred_element_type=F32)


def dot3(left, right, dims=NN):
    lh, ll = left
    rh, rl = right
    return dot(lh, rh, dims) + (dot(lh, rl, dims) + dot(ll, rh, dims))


def pair(ref, *index):
    return ref[(0,) + index], ref[(1,) + index]


def put(ref, value, *index):
    high, low = split(value)
    ref[(0,) + index] = high
    ref[(1,) + index] = low
    return high, low


ALL = slice(None)


def at(start, size, step=None):
    return pl.ds(pl.multiple_of(start, step or size), size)


def packed(value):
    high = value.astype(BF16).astype(F32)
    low = value - high
    first = lax.broadcasted_iota(jnp.int32, value.shape, 1) < HD
    high_r, low_r = pltpu.roll(high, HD, 1), pltpu.roll(low, HD, 1)
    hl = (jnp.where(first, high, low_r).astype(BF16), jnp.where(first, high_r, low).astype(BF16))
    lh = (jnp.where(first, low, high_r).astype(BF16), jnp.where(first, low_r, high).astype(BF16))
    return hl, lh


def kernel(
    nlist, ncount, tok, gain, wq, wk, wv, wo, cot,
    result, d_tokens, d_gain, d_q, d_k, d_v, d_o,
    xwin, wf, cotf, xhat, rstd, hid_t, w2, cot2, kp, vp, kt, vt, qp, dop, do_t, bias, dk2, dv2, dq2, o2,
    g, r0, r1, acc2, r2, acc3, r3, full, dhalo, halo_in, res_buf, dtok_buf, dg_acc,
    load_sem, tok_send, tok_recv, s0, q0, s1, q1, s2, q2, s3, q3, s4, q4, s5, q5, s6, q6, s7, q7,
    dh_send, dh_recv, out_sem,
):
    s = lax.axis_index("space")
    y = lax.axis_index("slab")
    count = NX * NZ * 2
    x, z, c = s // (2 * NZ), (s // 2) % NZ, s % 2
    partner = device(x, y, z, 1 - c)
    after = {"space": (s + 1) % count, "slab": y}
    before = {"space": (s + count - 1) % count, "slab": y}
    other = {"space": (s + count - 1 + 2 * c) % count, "slab": y}

    loads = [pltpu.make_async_copy(tok, xwin.at[pl.ds(ROWS, ROWS)], load_sem.at[0])]
    for i, ref in enumerate((wq, wk, wv, wo)):
        loads.append(pltpu.make_async_copy(ref, wf.at[i], load_sem.at[1 + i]))
    loads.append(pltpu.make_async_copy(cot, cotf, load_sem.at[5]))
    for load in loads:
        load.start()

    barrier = pltpu.get_barrier_semaphore()
    everyone = [partner, other]
    everyone += [device((x + d) % NX, y, z, c) for d in range(1, NX)]
    everyone += [device(x, (y + d) % NY, z, c) for d in range(1, NY)]
    everyone += [device(x, y, (z + d) % NZ, c) for d in range(1, NZ)]
    for peer in everyone:
        pl.semaphore_signal(barrier, inc=1, device_id=peer, device_id_type=MESH)
    pl.semaphore_wait(barrier, len(everyone))

    def remote(src, dst, send_sem, recv_sem, peer):
        return pltpu.make_async_remote_copy(src, dst, send_sem, recv_sem, device_id=peer, device_id_type=MESH)

    to_after = remote(tok, xwin.at[pl.ds(0, ROWS)], tok_send.at[0], tok_recv.at[0], after)
    to_before = remote(tok, xwin.at[pl.ds(2 * ROWS, ROWS)], tok_send.at[1], tok_recv.at[1], before)
    to_after.start()
    to_before.start()

    gain_row = gain[...]
    for w in range(6):
        for p in range(2):
            if w == 2 + p:
                flag = 0.0
            else:
                flag = -1e30
                for j in range(3):
                    live = jnp.logical_and(nlist[p, j] == w, j < ncount[p])
                    flag = jnp.where(live, 0.0, flag)
            bias[w * PT : (w + 1) * PT, p * PT : (p + 1) * PT] = jnp.full((PT, PT), flag, F32)

    def keys_values(block):
        rows = slice(block * ROWS, (block + 1) * ROWS)
        tokens = xwin[rows]
        centred = tokens - jnp.mean(tokens, axis=1, keepdims=True)
        inv = lax.rsqrt(jnp.mean(centred * centred, axis=1, keepdims=True) + 1e-5)
        hat = centred * inv
        xhat[rows] = hat
        rstd[rows] = inv
        hidden = hat * gain_row
        put(hid_t, hidden.T, ALL, rows)
        hidden2 = split(hidden)
        for i, pack, turned in ((1, kp, kt), (2, vp, vt)):
            value = dot3(hidden2, pair(w2.at[i], ALL, ALL))
            for hp in range(HEADS // 2):
                hl, _ = packed(value[:, hp * LANES : (hp + 1) * LANES])
                for half in range(2):
                    h = 2 * hp + half
                    pack[rows, h * LANES : (h + 1) * LANES] = hl[half]
            high, low = split(value.T)
            for h in range(HEADS):
                turned[h * LANES : h * LANES + HD, rows] = high[h * HD : (h + 1) * HD]
                turned[h * LANES + HD : (h + 1) * LANES, rows] = low[h * HD : (h + 1) * HD]
        return hidden2

    def pack_rows(pack, value):
        for hp in range(HEADS // 2):
            hl, lh = packed(value[:, hp * LANES : (hp + 1) * LANES])
            for half in range(2):
                h = 2 * hp + half
                pack[:, h * 2 * LANES : h * 2 * LANES + LANES] = hl[half]
                pack[:, h * 2 * LANES + LANES : (h + 1) * 2 * LANES] = lh[half]

    loads[0].wait()
    loads[2].wait()
    put(w2.at[1], wf[1], ALL, ALL)
    loads[3].wait()
    put(w2.at[2], wf[2], ALL, ALL)
    hidden2 = keys_values(1)
    loads[1].wait()
    put(w2.at[0], wf[0], ALL, ALL)
    pack_rows(qp, dot3(hidden2, pair(w2.at[0], ALL, ALL)) * HD**-0.5)
    loads[4].wait()
    put(w2.at[3], wf[3], ALL, ALL)
    loads[5].wait()
    put(cot2, cotf[...], ALL, ALL)
    d_mixed = dot3(pair(cot2, ALL, ALL), pair(w2.at[3], ALL, ALL), NT)
    pack_rows(dop, d_mixed)
    do_t[...] = d_mixed.T
    to_after.wait_recv()
    keys_values(0)
    to_before.wait_recv()
    keys_values(2)

    def axes(q):
        odd = q % 2
        even = 1 - odd
        one = x * even + y * odd
        two = x * odd + y * even

        def along_one(d):
            return device((x + d * even) % NX, (y + d * odd) % NY, z, c)

        def along_two(d):
            return device((x + d * odd) % NX, (y + d * even) % NY, z, c)

        return one, two, along_one, along_two

    def along_z(d):
        return device(x, y, (z + d) % NZ, c)

    def copies(level, q):
        one, two, along_one, along_two = axes(q)
        base1 = c * 1024 + one * 256
        base2 = base1 + two * 64
        if level == 0:
            return [remote(g.at[q, at((1 - c) * 1024, 1024)], r0.at[q], s0.at[q], q0.at[q], partner)]
        if level == 1:
            return [
                remote(
                    g.at[q, at(c * 1024 + ((one + d) % 4) * 256, 256)],
                    r1.at[q, d - 1], s1.at[q, d - 1], q1.at[q, d - 1], along_one(d),
                )
                for d in range(1, 4)
            ]
        if level == 2:
            return [
                remote(
                    acc2.at[q, at(((two + d) % 4) * 64, 64)],
                    r2.at[q, d - 1], s2.at[q, d - 1], q2.at[q, d - 1], along_two(d),
                )
                for d in range(1, 4)
            ]
        if level == 3:
            return [
                remote(
                    acc3.at[q, at(((z + d) % NZ) * 8, 8)],
                    r3.at[q, d - 1], s3.at[q, d - 1], q3.at[q, d - 1], along_z(d),
                )
                for d in range(1, 8)
            ]
        if level == 4:
            block = full.at[q, at(base2 + z * 8, 8)]
            return [remote(block, block, s4.at[q, d - 1], q4.at[q, d - 1], along_z(d)) for d in range(1, 8)]
        if level == 5:
            block = full.at[q, at(base2, 64)]
            return [remote(block, block, s5.at[q, d - 1], q5.at[q, d - 1], along_two(d)) for d in range(1, 4)]
        if level == 6:
            block = full.at[q, at(base1, 256)]
            return [remote(block, block, s6.at[q, d - 1], q6.at[q, d - 1], along_one(d)) for d in range(1, 4)]
        block = full.at[q, at(c * 1024, 1024)]
        return [remote(block, block, s7.at[q], q7.at[q], partner)]

    def go(level, q):
        for copy in copies(level, q):
            copy.start()

    def arrived(level, q):
        for copy in copies(level, q):
            copy.wait_recv()

    def step(level, q):
        one, two, _, _ = axes(q)
        base1 = c * 1024 + one * 256
        arrived(level - 1, q)
        if level == 1:
            mine = at(c * 1024, 1024)
            g[q, mine] = g[q, mine] + r0[q]
        elif level == 2:
            acc2[q] = (g[q, at(base1, 256)] + r1[q, 0]) + (r1[q, 1] + r1[q, 2])
        elif level == 3:
            acc3[q] = (acc2[q, at(two * 64, 64)] + r2[q, 0]) + (r2[q, 1] + r2[q, 2])
        elif level == 4:
            total = acc3[q, at(z * 8, 8)]
            for d in range(7):
                total = total + r3[q, d]
            full[q, at(base1 + two * 64 + z * 8, 8)] = total
        go(level, q)

    @pl.loop(0, QUARTERS)
    def _(hp):
        lanes = at(hp * LANES, LANES)
        first = lax.broadcasted_iota(jnp.int32, (WIN, LANES), 1) < HD
        sums_k, sums_v, mixed_ts, dq_ts = [], [], [], []
        for half in range(2):
            h = hp * 2 + half
            own = at(h * LANES, LANES)
            double = at(h * 2 * LANES, 2 * LANES)
            k_h, v_h = kp[:, own], vp[:, own]
            q_h, do_h = qp[:, double], dop[:, double]
            scores = dot(jnp.concatenate([k_h, k_h], axis=1), q_h, NT) + bias[...]
            weights = jnp.exp(scores - jnp.max(scores, axis=0, keepdims=True))
            prob = weights * (1.0 / jnp.sum(weights, axis=0, keepdims=True))
            p_high, p_low = split(prob)
            v_t = vt[own]
            both = dot(v_t, p_high) + dot(v_t, p_low)
            mixed_t = both[:HD] + both[HD:]
            mixed_ts.append(mixed_t)
            do_hl = do_h[:, :LANES]
            sum_v = dot(p_high, do_hl) + dot(p_low, do_hl)
            sums_v.append(sum_v + pltpu.roll(sum_v, HD, 1))
            d_prob = dot(jnp.concatenate([v_h, v_h], axis=1), do_h, NT)
            inner = jnp.sum(mixed_t * do_t[at(h * HD, HD)], axis=0, keepdims=True)
            ds_high, ds_low = split(prob * (d_prob - inner))
            k_t = kt[own]
            both = dot(k_t, ds_high) + dot(k_t, ds_low)
            dq_ts.append((both[:HD] + both[HD:]) * HD**-0.5)
            q_hl = q_h[:, :LANES]
            sum_k = dot(ds_high, q_hl) + dot(ds_low, q_hl)
            sums_k.append(sum_k + pltpu.roll(sum_k, HD, 1))
        dk_pair = put(dk2, jnp.where(first, sums_k[0], sums_k[1]), ALL, lanes)
        dv_pair = put(dv2, jnp.where(first, sums_v[0], sums_v[1]), ALL, lanes)
        dq_pair = put(dq2, jnp.concatenate(dq_ts, axis=0).T, ALL, lanes)
        mixed_t = jnp.concatenate(mixed_ts, axis=0)
        put(o2, mixed_t.T, ALL, lanes)
        kv = tuple(jnp.concatenate([a, b], axis=1) for a, b in zip(dk_pair, dv_pair))
        grad_kv = dot3(pair(hid_t, ALL, ALL), kv)
        g[hp, :D] = dot3(pair(hid_t, ALL, slice(ROWS, 2 * ROWS)), dq_pair)
        g[hp, D : 2 * D] = grad_kv[:, :LANES]
        g[hp, 2 * D : 3 * D] = grad_kv[:, LANES:]
        grad_o = dot3(split(mixed_t), pair(cot2, ALL, ALL))
        for i in range(4):
            g[hp, 3 * D + i * LANES : 3 * D + (i + 1) * LANES] = grad_o[:, i * LANES : (i + 1) * LANES]
        go(0, hp)
        for level in range(1, 4):

            @pl.when(hp >= level)
            def _(level=level):
                step(level, hp - level)

    def d_hidden(block):
        rows = slice(block * ROWS, (block + 1) * ROWS)
        part = dot3(pair(dk2, rows, ALL), pair(w2.at[1], ALL, ALL), NT)
        part = part + dot3(pair(dv2, rows, ALL), pair(w2.at[2], ALL, ALL), NT)
        if block == 1:
            part = part + dot3(pair(dq2, ALL, ALL), pair(w2.at[0], ALL, ALL), NT)
        grad = part * gain_row
        hat = xhat[rows]
        inner = jnp.mean(grad * hat, axis=1, keepdims=True)
        return rstd[rows] * (grad - jnp.mean(grad, axis=1, keepdims=True) - hat * inner)

    back = [
        remote(dhalo.at[0], halo_in.at[1], dh_send.at[0], dh_recv.at[0], before),
        remote(dhalo.at[1], halo_in.at[0], dh_send.at[1], dh_recv.at[1], after),
    ]
    outs = []

    def write(src, dst, sem):
        copy = pltpu.make_async_copy(src, dst, sem)
        copy.start()
        outs.append(copy)

    dhalo[0] = d_hidden(0)
    back[0].start()
    step(1, 3)
    step(2, 2)
    step(3, 1)
    step(4, 0)
    dhalo[1] = d_hidden(2)
    back[1].start()
    step(4, 1)
    step(3, 2)
    step(2, 3)
    step(5, 0)
    dtok_buf[...] = d_hidden(1) + cotf[...]
    step(4, 2)
    step(5, 1)
    step(3, 3)
    step(6, 0)
    res_buf[...] = dot3(pair(o2, ALL, ALL), pair(w2.at[3], ALL, ALL)) + xwin[ROWS : 2 * ROWS]
    write(res_buf, result, out_sem.at[0])
    step(5, 2)
    step(6, 1)
    step(4, 3)
    step(7, 0)
    step(6, 2)
    step(5, 3)
    step(7, 1)
    for copy in back:
        copy.wait_recv()
    dtok_buf[...] = dtok_buf[...] + (halo_in[0] + halo_in[1])
    write(dtok_buf, d_tokens, out_sem.at[1])
    dg_acc[...] = jnp.zeros_like(dg_acc)

    def finish(q):
        arrived(7, q)
        lanes = slice(q * LANES, (q + 1) * LANES)
        for i, ref in enumerate((d_q, d_k, d_v)):
            write(full.at[q, pl.ds(i * D, D)], ref.at[:, pl.ds(q * LANES, LANES)], out_sem.at[2 + q * 7 + i])
        for i in range(4):
            write(
                full.at[q, pl.ds(3 * D + i * LANES, LANES)],
                d_o.at[pl.ds(q * LANES, LANES), pl.ds(i * LANES, LANES)],
                out_sem.at[2 + q * 7 + 3 + i],
            )
        dg_acc[...] += (
            full[q, :D] * wf[0, :, lanes] + full[q, D : 2 * D] * wf[1, :, lanes] + full[q, 2 * D : 3 * D] * wf[2, :, lanes]
        )

    finish(0)
    step(6, 3)
    step(7, 2)
    finish(1)
    finish(2)
    step(7, 3)
    finish(3)
    d_gain[...] = jnp.broadcast_to(jnp.sum(dg_acc[...].T, axis=0, keepdims=True) / gain_row, d_gain.shape)
    to_after.wait_send()
    to_before.wait_send()
    for copy in back:
        copy.wait_send()
    for q in range(QUARTERS):
        for level in range(8):
            for copy in copies(level, q):
                copy.wait_send()
    for copy in outs:
        copy.wait()


def layer(nlist, ncount, tokens, gain, wq, wk, wv, wo, cot):
    vmem = pl.BlockSpec(memory_space=pltpu.VMEM)
    smem = pl.BlockSpec(memory_space=pltpu.SMEM)
    hbm = pl.BlockSpec(memory_space=pl.ANY)
    shape = jax.ShapeDtypeStruct
    dma = pltpu.SemaphoreType.DMA
    v = pltpu.VMEM
    wide = HEADS * LANES
    scratch = [
        v((WIN, D), F32),
        v((4, D, D), F32),
        v((ROWS, D), F32),
        v((WIN, D), F32),
        v((WIN, 1), F32),
        v((2, D, WIN), BF16),
        v((4, 2, D, D), BF16),
        v((2, ROWS, D), BF16),
        v((WIN, wide), BF16),
        v((WIN, wide), BF16),
        v((wide, WIN), BF16),
        v((wide, WIN), BF16),
        v((ROWS, 2 * wide), BF16),
        v((ROWS, 2 * wide), BF16),
        v((D, ROWS), F32),
        v((WIN, ROWS), F32),
        v((2, WIN, D), BF16),
        v((2, WIN, D), BF16),
        v((2, ROWS, D), BF16),
        v((2, ROWS, D), BF16),
        v((4, 2048, LANES), F32),
        v((4, 1024, LANES), F32),
        v((4, 3, 256, LANES), F32),
        v((4, 256, LANES), F32),
        v((4, 3, 64, LANES), F32),
        v((4, 64, LANES), F32),
        v((4, 7, 8, LANES), F32),
        v((4, 2048, LANES), F32),
        v((2, ROWS, D), F32),
        v((2, ROWS, D), F32),
        v((ROWS, D), F32),
        v((ROWS, D), F32),
        v((D, LANES), F32),
        dma((6,)),
        dma((2,)),
        dma((2,)),
    ]
    for peers in ((4,), (4, 3), (4, 3), (4, 7), (4, 7), (4, 3), (4, 3), (4,)):
        scratch += [dma(peers), dma(peers)]
    scratch += [dma((2,)), dma((2,)), dma((30,))]
    return pl.pallas_call(
        kernel,
        out_shape=(
            shape((ROWS, D), F32),
            shape((ROWS, D), F32),
            shape((8, D), F32),
            shape((D, D), F32),
            shape((D, D), F32),
            shape((D, D), F32),
            shape((D, D), F32),
        ),
        in_specs=[smem] * 2 + [hbm, vmem] + [hbm] * 5,
        out_specs=(hbm, hbm, vmem, hbm, hbm, hbm, hbm),
        scratch_shapes=scratch,
        compiler_params=pltpu.CompilerParams(
            collective_id=0, has_side_effects=True, vmem_limit_bytes=60 << 20
        ),
        name="patch_layer",
    )(nlist, ncount, tokens, gain, wq, wk, wv, wo, cot)


def body(tokens, gain, wq, wk, wv, wo, nlist, ncount, cot):
    result, d_tokens, d_gain, d_q, d_k, d_v, d_o = layer(
        nlist, ncount, tokens, gain[None, :], wq, wk, wv, wo, cot
    )
    return (result, d_tokens, d_gain[0], d_q, d_k, d_v, d_o)


def solution(mesh):
    rows = P(("space", "slab"), None)
    return jax.shard_map(
        body,
        mesh=mesh,
        in_specs=(rows, P(), P(), P(), P(), P(), rows, P(("space", "slab")), rows),
        out_specs=(rows, rows, P(), P(), P(), P(), P()),
        check_vma=False,
    )
```

time: 436 us -> 110 us (0.25); the launches traced: 428 us -> 110 us
  waiting for transfers between devices: 178 us -> 0 us
  Pallas kernels: 0 us -> 99.1 us
  blocking collectives: 78.4 us -> 0 us
  matrix products: 63.4 us -> 0 us
  local copies, waits for them, and re-layouts: 56.7 us -> 9.89 us
  other arithmetic: 22.6 us -> 0 us
  between operations: 14.9 us -> 0.66 us
  starting transfers between devices: 14.1 us -> 0 us
    psum x1 -> x0, waiting for transfers between devices: 177 us -> none  [body(): lax.psum((grad_gain, grad_query, grad_key, grad_value, grad_output), ('sp...]
    pallas_call x0 -> x1, Pallas kernels: none -> 99.1 us  [layer(): pl.pallas_call(kernel, out_shape=(shape((ROWS, D), F32), shape((ROWS, D),...]
    psum x1 -> x0, blocking collectives: 78.4 us -> none  [body(): lax.psum((grad_gain, grad_query, grad_key, grad_value, grad_output), ('sp...]
    dot_general x18 -> x0, matrix products: 63.4 us -> none  [the longest x12 30.5 us: matmul(): jnp.dot(left, right, precision=lax.Precision.HIGHEST, preferred_element_t...]
    reshape x10 -> x0, local copies, waits for them, and re-layouts: 38.4 us -> none  [the longest x4 17.3 us: attention(): value_win.reshape(-1, PT, model_width)[block_index]]
    ppermute x4 -> x0, starting transfers between devices: 14.1 us -> none  [the longest x2 10.8 us: passed_along(): return lax.ppermute(value, axis, pairs)]
    scatter-add x2 -> x0, other arithmetic: 8.39 us -> none  [the longest x1 5.02 us: attention(): key_win.reshape(-1, PT, model_width)[block_index]]
    reduce_sum x5 -> x0, other arithmetic: 7.29 us -> none  [the longest x1 2.16 us: attention(): weights = jnp.exp(scores - row_max)]
  transfers between devices with their start and end apart: 5 -> 0, of which waited for: 2 -> 0; matrix products, arithmetic and copies ran while one was open for 10% -> 0% of each run, Pallas kernels for 0% -> 0%
where the time goes in v2:
time: 110 us
  Pallas kernels  99.1 us (90%)
  local copies, waits for them, and re-layouts  9.89 us (9%)
    pallas_call x1, Pallas kernels, layer(): pl.pallas_call(kernel, out_shape=(shape((ROWS, D), F32), shape((ROWS, D),...  99.1 us
    unnamed x16, local copies, waits for them, and re-layouts  8.53 us

profile of v2, /device:TPU:1, one launch (start us, length us, event | category | flops | bytes accessed | tf_op | source)
XLA Modules:
  0.0 109.7 jit_solution(17965095509266432438)
XLA Ops:
  0.6 99.1 %patch_layer.1 = (f32[256,512]{1,0:T(8,128)}, f32[256,512]{1,0:T(8,128)}, f32[8,512]{1,0:T(8,128)}, f32[512,512]{1,0:T(8,128)}, f32[512,512]{1,0:T(8,128)}, /*index=5*/f32[512,512]{1,0:T(8,128)}, f32[512,512]{1,0:T(8,128)}) custom-call(s32[2,3]{1,0:T(2,128)} %nlist.1, s32[2]{0:T(128)} %ncount.1, f32[256,512]{1,0:T(8,128)} %tok.1, f32[1,512]{1,0:T(1,128)} %bitcast.2, ...), custom_call_target="tpu_custom_call" | custom-call | tf_op jit(solution)/shard_map/patch_layer/pallas_call | solution.py:452
  99.8 0.0 copy-start.4
  99.8 1.4 %slice.3 = f32[1,512]{1,0:T(1,128)} slice(f32[8,512]{1,0:T(8,128)} %get-tuple-element.16), slice={[0:1], [0:512]} | slice | bytes 4096 | tf_op jit(solution)/shard_map/slice | solution.py:477
  101.1 0.0 copy-start.3
  101.1 2.0 %copy.22 = f32[256,512]{1,0:T(8,128)} copy(f32[256,512]{1,0:T(8,128)} %get-tuple-element.28) | data formatting | bytes 1048576
  103.1 0.0 copy-done.4
  103.1 0.8 copy.23
  103.9 0.0 copy-done.3
  103.9 0.0 copy-start.2
  103.9 1.0 copy.24
  104.9 0.6 copy-done.2
  105.5 0.0 copy-start.1
  105.5 1.0 copy.25
  106.5 0.6 copy-done.1
  107.1 0.0 copy-start
  107.1 1.0 copy.26
  108.1 0.6 copy-done
  108.7 1.0 copy.27
Async XLA Ops:
  99.8 3.3 %copy-start.4 = (f32[256,512]{1,0:T(8,128)S(1)}, f32[256,512]{1,0:T(8,128)}, u32[]{:S(2)}) copy-start(f32[256,512]{1,0:T(8,128)} %get-tuple-element.29) | copy-start | bytes 1572868
  101.1 2.8 %copy-start.3 = (f32[512,512]{1,0:T(8,128)S(1)}, f32[512,512]{1,0:T(8,128)}, u32[]{:S(2)}) copy-start(f32[512,512]{1,0:T(8,128)} %get-tuple-element.31) | copy-start | bytes 3145732
  103.9 1.6 %copy-start.2 = (f32[512,512]{1,0:T(8,128)S(1)}, f32[512,512]{1,0:T(8,128)}, u32[]{:S(2)}) copy-start(f32[512,512]{1,0:T(8,128)} %get-tuple-element.32) | copy-start | bytes 3145732
  105.5 1.6 %copy-start.1 = (f32[512,512]{1,0:T(8,128)S(1)}, f32[512,512]{1,0:T(8,128)}, u32[]{:S(2)}) copy-start(f32[512,512]{1,0:T(8,128)} %get-tuple-element.33) | copy-start | bytes 3145732
  107.1 1.6 %copy-start = (f32[512,512]{1,0:T(8,128)S(1)}, f32[512,512]{1,0:T(8,128)}, u32[]{:S(2)}) copy-start(f32[512,512]{1,0:T(8,128)} %get-tuple-element.34) | copy-start | bytes 3145732

commit v3 on v2

--- a/solution.py
+++ b/solution.py
@@ -175,64 +175,58 @@
     to_before.wait_recv()
     keys_values(2)
 
-    def axes(q):
-        odd = q % 2
-        even = 1 - odd
-        one = x * even + y * odd
-        two = x * odd + y * even
-
-        def along_one(d):
-            return device((x + d * even) % NX, (y + d * odd) % NY, z, c)
-
-        def along_two(d):
-            return device((x + d * odd) % NX, (y + d * even) % NY, z, c)
-
-        return one, two, along_one, along_two
+    half_a = c * 1024
+    half_b = half_a + 512
+    x_rows, y_rows = half_a + x * 128, half_b + y * 128
+    xy_rows, yx_rows = x_rows + y * 32, y_rows + x * 32
+    upper = z // 4
+    tile = xy_rows * (1 - upper) + yx_rows * upper + (z % 4) * 8
+
+    def along_x(d):
+        return device((x + d) % NX, y, z, c)
+
+    def along_y(d):
+        return device(x, (y + d) % NY, z, c)
 
     def along_z(d):
         return device(x, y, (z + d) % NZ, c)
 
     def copies(level, q):
-        one, two, along_one, along_two = axes(q)
-        base1 = c * 1024 + one * 256
-        base2 = base1 + two * 64
         if level == 0:
             return [remote(g.at[q, at((1 - c) * 1024, 1024)], r0.at[q], s0.at[q], q0.at[q], partner)]
-        if level == 1:
-            return [
-                remote(
-                    g.at[q, at(c * 1024 + ((one + d) % 4) * 256, 256)],
-                    r1.at[q, d - 1], s1.at[q, d - 1], q1.at[q, d - 1], along_one(d),
-                )
-                for d in range(1, 4)
-            ]
-        if level == 2:
-            return [
-                remote(
-                    acc2.at[q, at(((two + d) % 4) * 64, 64)],
-                    r2.at[q, d - 1], s2.at[q, d - 1], q2.at[q, d - 1], along_two(d),
-                )
-                for d in range(1, 4)
-            ]
+        if level == 7:
+            block = full.at[q, at(c * 1024, 1024)]
+            return [remote(block, block, s7.at[q], q7.at[q], partner)]
         if level == 3:
             return [
-                remote(
-                    acc3.at[q, at(((z + d) % NZ) * 8, 8)],
-                    r3.at[q, d - 1], s3.at[q, d - 1], q3.at[q, d - 1], along_z(d),
-                )
-                for d in range(1, 8)
+                remote(acc3.at[q, at(((z + d) % NZ) * 8, 8)], r3.at[q, d - 1], s3.at[q, d - 1], q3.at[q, d - 1], along_z(d))
+                for d in range(1, NZ)
             ]
         if level == 4:
-            block = full.at[q, at(base2 + z * 8, 8)]
-            return [remote(block, block, s4.at[q, d - 1], q4.at[q, d - 1], along_z(d)) for d in range(1, 8)]
-        if level == 5:
-            block = full.at[q, at(base2, 64)]
-            return [remote(block, block, s5.at[q, d - 1], q5.at[q, d - 1], along_two(d)) for d in range(1, 4)]
-        if level == 6:
-            block = full.at[q, at(base1, 256)]
-            return [remote(block, block, s6.at[q, d - 1], q6.at[q, d - 1], along_one(d)) for d in range(1, 4)]
-        block = full.at[q, at(c * 1024, 1024)]
-        return [remote(block, block, s7.at[q], q7.at[q], partner)]
+            block = full.at[q, at(tile, 8)]
+            return [remote(block, block, s4.at[q, d - 1], q4.at[q, d - 1], along_z(d)) for d in range(1, NZ)]
+        found = []
+        for d in range(1, 4):
+            xd, yd = (x + d) % NX, (y + d) % NY
+            if level == 1:
+                a = (g.at[q, at(half_a + xd * 128, 128)], r1.at[q, 0, d - 1], along_x(d))
+                b = (g.at[q, at(half_b + yd * 128, 128)], r1.at[q, 1, d - 1], along_y(d))
+                ss, rs = s1, q1
+            elif level == 2:
+                a = (acc2.at[q, 0, at(yd * 32, 32)], r2.at[q, 0, d - 1], along_y(d))
+                b = (acc2.at[q, 1, at(xd * 32, 32)], r2.at[q, 1, d - 1], along_x(d))
+                ss, rs = s2, q2
+            elif level == 5:
+                a = (full.at[q, at(xy_rows, 32)], full.at[q, at(xy_rows, 32)], along_y(d))
+                b = (full.at[q, at(yx_rows, 32)], full.at[q, at(yx_rows, 32)], along_x(d))
+                ss, rs = s5, q5
+            else:
+                a = (full.at[q, at(x_rows, 128)], full.at[q, at(x_rows, 128)], along_x(d))
+                b = (full.at[q, at(y_rows, 128)], full.at[q, at(y_rows, 128)], along_y(d))
+                ss, rs = s6, q6
+            for i, (src, dst, peer) in enumerate((a, b)):
+                found.append(remote(src, dst, ss.at[q, i * 3 + d - 1], rs.at[q, i * 3 + d - 1], peer))
+        return found
 
     def go(level, q):
         for copy in copies(level, q):
@@ -243,21 +237,21 @@
             copy.wait_recv()
 
     def step(level, q):
-        one, two, _, _ = axes(q)
-        base1 = c * 1024 + one * 256
         arrived(level - 1, q)
         if level == 1:
             mine = at(c * 1024, 1024)
             g[q, mine] = g[q, mine] + r0[q]
         elif level == 2:
-            acc2[q] = (g[q, at(base1, 256)] + r1[q, 0]) + (r1[q, 1] + r1[q, 2])
+            for i, rows in enumerate((x_rows, y_rows)):
+                acc2[q, i] = (g[q, at(rows, 128)] + r1[q, i, 0]) + (r1[q, i, 1] + r1[q, i, 2])
         elif level == 3:
-            acc3[q] = (acc2[q, at(two * 64, 64)] + r2[q, 0]) + (r2[q, 1] + r2[q, 2])
+            for i, row in enumerate((y * 32, x * 32)):
+                acc3[q, i * 32 : i * 32 + 32] = (acc2[q, i, at(row, 32)] + r2[q, i, 0]) + (r2[q, i, 1] + r2[q, i, 2])
         elif level == 4:
             total = acc3[q, at(z * 8, 8)]
             for d in range(7):
                 total = total + r3[q, d]
-            full[q, at(base1 + two * 64 + z * 8, 8)] = total
+            full[q, at(tile, 8)] = total
         go(level, q)
 
     @pl.loop(0, QUARTERS)
@@ -291,6 +285,12 @@
             q_hl = q_h[:, :LANES]
             sum_k = dot(ds_high, q_hl) + dot(ds_low, q_hl)
             sums_k.append(sum_k + pltpu.roll(sum_k, HD, 1))
+            if half == 0:
+
+                @pl.when(hp >= 1)
+                def _():
+                    step(1, hp - 1)
+
         dk_pair = put(dk2, jnp.where(first, sums_k[0], sums_k[1]), ALL, lanes)
         dv_pair = put(dv2, jnp.where(first, sums_v[0], sums_v[1]), ALL, lanes)
         dq_pair = put(dq2, jnp.concatenate(dq_ts, axis=0).T, ALL, lanes)
@@ -305,7 +305,7 @@
         for i in range(4):
             g[hp, 3 * D + i * LANES : 3 * D + (i + 1) * LANES] = grad_o[:, i * LANES : (i + 1) * LANES]
         go(0, hp)
-        for level in range(1, 4):
+        for level in range(2, 4):
 
             @pl.when(hp >= level)
             def _(level=level):
@@ -332,38 +332,6 @@
         copy = pltpu.make_async_copy(src, dst, sem)
         copy.start()
         outs.append(copy)
-
-    dhalo[0] = d_hidden(0)
-    back[0].start()
-    step(1, 3)
-    step(2, 2)
-    step(3, 1)
-    step(4, 0)
-    dhalo[1] = d_hidden(2)
-    back[1].start()
-    step(4, 1)
-    step(3, 2)
-    step(2, 3)
-    step(5, 0)
-    dtok_buf[...] = d_hidden(1) + cotf[...]
-    step(4, 2)
-    step(5, 1)
-    step(3, 3)
-    step(6, 0)
-    res_buf[...] = dot3(pair(o2, ALL, ALL), pair(w2.at[3], ALL, ALL)) + xwin[ROWS : 2 * ROWS]
-    write(res_buf, result, out_sem.at[0])
-    step(5, 2)
-    step(6, 1)
-    step(4, 3)
-    step(7, 0)
-    step(6, 2)
-    step(5, 3)
-    step(7, 1)
-    for copy in back:
-        copy.wait_recv()
-    dtok_buf[...] = dtok_buf[...] + (halo_in[0] + halo_in[1])
-    write(dtok_buf, d_tokens, out_sem.at[1])
-    dg_acc[...] = jnp.zeros_like(dg_acc)
 
     def finish(q):
         arrived(7, q)
@@ -380,14 +348,45 @@
             full[q, :D] * wf[0, :, lanes] + full[q, D : 2 * D] * wf[1, :, lanes] + full[q, 2 * D : 3 * D] * wf[2, :, lanes]
         )
 
+    dhalo[0] = d_hidden(0)
+    step(1, 3)
+    step(2, 2)
+    step(3, 1)
+    step(4, 0)
+    dhalo[1] = d_hidden(2)
+    step(3, 2)
+    step(2, 3)
+    step(4, 1)
+    step(5, 0)
+    dtok_buf[...] = d_hidden(1) + cotf[...]
+    step(3, 3)
+    step(4, 2)
+    step(5, 1)
+    step(6, 0)
+    res_buf[...] = dot3(pair(o2, ALL, ALL), pair(w2.at[3], ALL, ALL)) + xwin[ROWS : 2 * ROWS]
+    write(res_buf, result, out_sem.at[0])
+    dg_acc[...] = jnp.zeros_like(dg_acc)
+    step(4, 3)
+    step(5, 2)
+    step(6, 1)
+    step(7, 0)
+    step(6, 2)
+    step(5, 3)
+    back[0].start()
+    back[1].start()
+    step(7, 1)
+    step(6, 3)
     finish(0)
-    step(6, 3)
     step(7, 2)
     finish(1)
+    for copy in back:
+        copy.wait_recv()
+    dtok_buf[...] = dtok_buf[...] + (halo_in[0] + halo_in[1])
+    write(dtok_buf, d_tokens, out_sem.at[1])
+    step(7, 3)
     finish(2)
-    step(7, 3)
     finish(3)
-    d_gain[...] = jnp.broadcast_to(jnp.sum(dg_acc[...].T, axis=0, keepdims=True) / gain_row, d_gain.shape)
+    d_gain[...] = jnp.sum(dg_acc[...].T, axis=0, keepdims=True) / gain_row
     to_after.wait_send()
     to_before.wait_send()
     for copy in back:
@@ -431,9 +430,9 @@
         v((2, ROWS, D), BF16),
         v((4, 2048, LANES), F32),
         v((4, 1024, LANES), F32),
-        v((4, 3, 256, LANES), F32),
-        v((4, 256, LANES), F32),
-        v((4, 3, 64, LANES), F32),
+        v((4, 2, 3, 128, LANES), F32),
+        v((4, 2, 128, LANES), F32),
+        v((4, 2, 3, 32, LANES), F32),
         v((4, 64, LANES), F32),
         v((4, 7, 8, LANES), F32),
         v((4, 2048, LANES), F32),
@@ -446,7 +445,7 @@
         dma((2,)),
         dma((2,)),
     ]
-    for peers in ((4,), (4, 3), (4, 3), (4, 7), (4, 7), (4, 3), (4, 3), (4,)):
+    for peers in ((4,), (4, 6), (4, 6), (4, 7), (4, 7), (4, 6), (4, 6), (4,)):
         scratch += [dma(peers), dma(peers)]
     scratch += [dma((2,)), dma((2,)), dma((30,))]
     return pl.pallas_call(
@@ -454,7 +453,7 @@
         out_shape=(
             shape((ROWS, D), F32),
             shape((ROWS, D), F32),
-            shape((8, D), F32),
+            shape((1, D), F32),
             shape((D, D), F32),
             shape((D, D), F32),
             shape((D, D), F32),
@@ -470,10 +469,47 @@
     )(nlist, ncount, tokens, gain, wq, wk, wv, wo, cot)
 
 
+PARTS = 4
+
+
+def write_kernel(*refs):
+    arrays = (len(refs) - 2) // 3
+    load_sem, store_sem = refs[-2:]
+    loads, stores = [], []
+    for i in range(arrays):
+        src, dst, buf = refs[i], refs[arrays + i], refs[2 * arrays + i]
+        rows = src.shape[0]
+        parts = PARTS if rows >= 8 * PARTS else 1
+        for j in range(parts):
+            block = pl.ds(j * (rows // parts), rows // parts)
+            loads.append(pltpu.make_async_copy(src.at[block], buf.at[block], load_sem.at[i, j]))
+            stores.append(pltpu.make_async_copy(buf.at[block], dst.at[block], store_sem.at[i, j]))
+    for load in loads:
+        load.start()
+    for load, store in zip(loads, stores):
+        load.wait()
+        store.start()
+    for store in stores:
+        store.wait()
+
+
+def written(*arrays):
+    hbm = pl.BlockSpec(memory_space=pl.ANY)
+    sems = pltpu.SemaphoreType.DMA((len(arrays), PARTS))
+    return pl.pallas_call(
+        write_kernel,
+        out_shape=tuple(jax.ShapeDtypeStruct(a.shape, a.dtype) for a in arrays),
+        in_specs=[hbm] * len(arrays),
+        out_specs=(hbm,) * len(arrays),
+        scratch_shapes=[pltpu.VMEM(a.shape, a.dtype) for a in arrays] + [sems, sems],
+        compiler_params=pltpu.CompilerParams(vmem_limit_bytes=60 << 20),
+        name="write_results",
+    )(*arrays)
+
+
 def body(tokens, gain, wq, wk, wv, wo, nlist, ncount, cot):
-    result, d_tokens, d_gain, d_q, d_k, d_v, d_o = layer(
-        nlist, ncount, tokens, gain[None, :], wq, wk, wv, wo, cot
-    )
+    results = layer(nlist, ncount, tokens, gain[None, :], wq, wk, wv, wo, cot)
+    result, d_tokens, d_gain, d_q, d_k, d_v, d_o = written(*results)
     return (result, d_tokens, d_gain[0], d_q, d_k, d_v, d_o)
 
 

time: 110 us -> 91.9 us (0.84)
  local copies, waits for them, and re-layouts: 9.89 us -> 0 us
  Pallas kernels: 99.1 us -> 91 us
    pallas_call x1, Pallas kernels: 99.1 us -> 86 us  [layer(): pl.pallas_call(kernel, out_shape=(shape((ROWS, D), F32), shape((ROWS, D),...]
    unnamed x16 -> x0, local copies, waits for them, and re-layouts: 8.53 us -> none
    pallas_call x0 -> x1, Pallas kernels: none -> 5.08 us  [written(): pl.pallas_call(write_kernel, out_shape=tuple((jax.ShapeDtypeStruct(a.shap...]
    slice x1 -> x0, local copies, waits for them, and re-layouts: 1.35 us -> none  [body(): return (result, d_tokens, d_gain[0], d_q, d_k, d_v, d_o)]
where the time goes in v3:
time: 91.9 us; the launch traced here: 91.8 us
  Pallas kernels  91 us (99%)
    pallas_call x1, Pallas kernels, layer(): pl.pallas_call(kernel, out_shape=(shape((ROWS, D), F32), shape((ROWS, D),...  86 us
    pallas_call x1, Pallas kernels, written(): pl.pallas_call(write_kernel, out_shape=tuple((jax.ShapeDtypeStruct(a.shap...  5.08 us

profile of v3, /device:TPU:1, one launch (start us, length us, event | category | flops | bytes accessed | tf_op | source)
XLA Modules:
  0.0 91.8 jit_solution(2598248336369075745)
XLA Ops:
  0.6 86.0 %patch_layer.1 = (f32[256,512]{1,0:T(8,128)}, f32[256,512]{1,0:T(8,128)}, f32[1,512]{1,0:T(1,128)}, f32[512,512]{1,0:T(8,128)}, f32[512,512]{1,0:T(8,128)}, /*index=5*/f32[512,512]{1,0:T(8,128)}, f32[512,512]{1,0:T(8,128)}) custom-call(s32[2,3]{1,0:T(2,128)} %nlist.1, s32[2]{0:T(128)} %ncount.1, f32[256,512]{1,0:T(8,128)} %tok.1, f32[1,512]{1,0:T(1,128)} %bitcast.2, ...), custom_call_target="tpu_custom_call" | custom-call | tf_op jit(solution)/shard_map/patch_layer/pallas_call | solution.py:451
  86.6 5.1 %write_results.1 = (f32[256,512]{1,0:T(8,128)}, f32[256,512]{1,0:T(8,128)}, f32[1,512]{1,0:T(1,128)}, f32[512,512]{1,0:T(8,128)}, f32[512,512]{1,0:T(8,128)}, /*index=5*/f32[512,512]{1,0:T(8,128)}, f32[512,512]{1,0:T(8,128)}) custom-call(f32[256,512]{1,0:T(8,128)} %get-tuple-element.21.refs_0_, f32[256,512]{1,0:T(8,128)} %get-tuple-element.22.refs_1_, ...), custom_call_target="tpu_custom_call" | custom-call | tf_op jit(solution)/shard_map/write_results/pallas_call | solution.py:499

commit v4 on v3

--- a/solution.py
+++ b/solution.py
@@ -74,19 +74,22 @@
     result, d_tokens, d_gain, d_q, d_k, d_v, d_o,
     xwin, wf, cotf, xhat, rstd, hid_t, w2, cot2, kp, vp, kt, vt, qp, dop, do_t, bias, dk2, dv2, dq2, o2,
     g, r0, r1, acc2, r2, acc3, r3, full, dhalo, halo_in, res_buf, dtok_buf, dg_acc,
-    load_sem, tok_send, tok_recv, s0, q0, s1, q1, s2, q2, s3, q3, s4, q4, s5, q5, s6, q6, s7, q7,
-    dh_send, dh_recv, out_sem,
+    load_sem, tok_send, tok_recv, level_send, level_recv, dh_send, dh_recv, out_sem,
 ):
     s = lax.axis_index("space")
     y = lax.axis_index("slab")
     count = NX * NZ * 2
     x, z, c = s // (2 * NZ), (s // 2) % NZ, s % 2
     partner = device(x, y, z, 1 - c)
-    after = {"space": (s + 1) % count, "slab": y}
-    before = {"space": (s + count - 1) % count, "slab": y}
     other = {"space": (s + count - 1 + 2 * c) % count, "slab": y}
-
-    loads = [pltpu.make_async_copy(tok, xwin.at[pl.ds(ROWS, ROWS)], load_sem.at[0])]
+    xs = [(x + d) % NX for d in range(NX)]
+    ys = [(y + d) % NY for d in range(NY)]
+    zs = [(z + d) % NZ for d in range(NZ)]
+    along_x = [device(i, y, z, c) for i in xs]
+    along_y = [device(x, i, z, c) for i in ys]
+    along_z = [device(x, y, i, c) for i in zs]
+
+    loads = [pltpu.make_async_copy(tok, xwin.at[pl.ds(0, ROWS)], load_sem.at[0])]
     for i, ref in enumerate((wq, wk, wv, wo)):
         loads.append(pltpu.make_async_copy(ref, wf.at[i], load_sem.at[1 + i]))
     loads.append(pltpu.make_async_copy(cot, cotf, load_sem.at[5]))
@@ -94,10 +97,7 @@
         load.start()
 
     barrier = pltpu.get_barrier_semaphore()
-    everyone = [partner, other]
-    everyone += [device((x + d) % NX, y, z, c) for d in range(1, NX)]
-    everyone += [device(x, (y + d) % NY, z, c) for d in range(1, NY)]
-    everyone += [device(x, y, (z + d) % NZ, c) for d in range(1, NZ)]
+    everyone = [partner, other] + along_x[1:] + along_y[1:] + along_z[1:]
     for peer in everyone:
         pl.semaphore_signal(barrier, inc=1, device_id=peer, device_id_type=MESH)
     pl.semaphore_wait(barrier, len(everyone))
@@ -105,22 +105,23 @@
     def remote(src, dst, send_sem, recv_sem, peer):
         return pltpu.make_async_remote_copy(src, dst, send_sem, recv_sem, device_id=peer, device_id_type=MESH)
 
-    to_after = remote(tok, xwin.at[pl.ds(0, ROWS)], tok_send.at[0], tok_recv.at[0], after)
-    to_before = remote(tok, xwin.at[pl.ds(2 * ROWS, ROWS)], tok_send.at[1], tok_recv.at[1], before)
-    to_after.start()
-    to_before.start()
+    to_far = remote(tok, xwin.at[pl.ds(2 * ROWS, ROWS)], tok_send.at[1], tok_recv.at[1], other)
+    to_near = remote(tok, xwin.at[pl.ds(ROWS, ROWS)], tok_send.at[0], tok_recv.at[0], partner)
+    to_far.start()
+    to_near.start()
 
     gain_row = gain[...]
-    for w in range(6):
+    for b in range(6):
+        name = (2, 4 * (1 - c), 4 * c)[b // 2] + b % 2
         for p in range(2):
-            if w == 2 + p:
+            if b == p:
                 flag = 0.0
             else:
                 flag = -1e30
                 for j in range(3):
-                    live = jnp.logical_and(nlist[p, j] == w, j < ncount[p])
+                    live = jnp.logical_and(nlist[p, j] == name, j < ncount[p])
                     flag = jnp.where(live, 0.0, flag)
-            bias[w * PT : (w + 1) * PT, p * PT : (p + 1) * PT] = jnp.full((PT, PT), flag, F32)
+            bias[b * PT : (b + 1) * PT, p * PT : (p + 1) * PT] = jnp.full((PT, PT), flag, F32)
 
     def keys_values(block):
         rows = slice(block * ROWS, (block + 1) * ROWS)
@@ -159,7 +160,7 @@
     put(w2.at[1], wf[1], ALL, ALL)
     loads[3].wait()
     put(w2.at[2], wf[2], ALL, ALL)
-    hidden2 = keys_values(1)
+    hidden2 = keys_values(0)
     loads[1].wait()
     put(w2.at[0], wf[0], ALL, ALL)
     pack_rows(qp, dot3(hidden2, pair(w2.at[0], ALL, ALL)) * HD**-0.5)
@@ -170,9 +171,9 @@
     d_mixed = dot3(pair(cot2, ALL, ALL), pair(w2.at[3], ALL, ALL), NT)
     pack_rows(dop, d_mixed)
     do_t[...] = d_mixed.T
-    to_after.wait_recv()
-    keys_values(0)
-    to_before.wait_recv()
+    to_near.wait_recv()
+    keys_values(1)
+    to_far.wait_recv()
     keys_values(2)
 
     half_a = c * 1024
@@ -182,62 +183,49 @@
     upper = z // 4
     tile = xy_rows * (1 - upper) + yx_rows * upper + (z % 4) * 8
 
-    def along_x(d):
-        return device((x + d) % NX, y, z, c)
-
-    def along_y(d):
-        return device(x, (y + d) % NY, z, c)
-
-    def along_z(d):
-        return device(x, y, (z + d) % NZ, c)
-
     def copies(level, q):
         if level == 0:
-            return [remote(g.at[q, at((1 - c) * 1024, 1024)], r0.at[q], s0.at[q], q0.at[q], partner)]
+            return [(g.at[q, at((1 - c) * 1024, 1024)], r0.at[q], partner)]
         if level == 7:
-            block = full.at[q, at(c * 1024, 1024)]
-            return [remote(block, block, s7.at[q], q7.at[q], partner)]
+            return [(full.at[q, at(c * 1024, 1024)], full.at[q, at(c * 1024, 1024)], partner)]
         if level == 3:
-            return [
-                remote(acc3.at[q, at(((z + d) % NZ) * 8, 8)], r3.at[q, d - 1], s3.at[q, d - 1], q3.at[q, d - 1], along_z(d))
-                for d in range(1, NZ)
-            ]
+            return [(acc3.at[q, at(zs[d] * 8, 8)], r3.at[q, d - 1], along_z[d]) for d in range(1, NZ)]
         if level == 4:
-            block = full.at[q, at(tile, 8)]
-            return [remote(block, block, s4.at[q, d - 1], q4.at[q, d - 1], along_z(d)) for d in range(1, NZ)]
+            return [(full.at[q, at(tile, 8)], full.at[q, at(tile, 8)], along_z[d]) for d in range(1, NZ)]
         found = []
         for d in range(1, 4):
-            xd, yd = (x + d) % NX, (y + d) % NY
             if level == 1:
-                a = (g.at[q, at(half_a + xd * 128, 128)], r1.at[q, 0, d - 1], along_x(d))
-                b = (g.at[q, at(half_b + yd * 128, 128)], r1.at[q, 1, d - 1], along_y(d))
-                ss, rs = s1, q1
+                found.append((g.at[q, at(half_a + xs[d] * 128, 128)], r1.at[q, 0, d - 1], along_x[d]))
+                found.append((g.at[q, at(half_b + ys[d] * 128, 128)], r1.at[q, 1, d - 1], along_y[d]))
             elif level == 2:
-                a = (acc2.at[q, 0, at(yd * 32, 32)], r2.at[q, 0, d - 1], along_y(d))
-                b = (acc2.at[q, 1, at(xd * 32, 32)], r2.at[q, 1, d - 1], along_x(d))
-                ss, rs = s2, q2
+                found.append((acc2.at[q, 0, at(ys[d] * 32, 32)], r2.at[q, 0, d - 1], along_y[d]))
+                found.append((acc2.at[q, 1, at(xs[d] * 32, 32)], r2.at[q, 1, d - 1], along_x[d]))
             elif level == 5:
-                a = (full.at[q, at(xy_rows, 32)], full.at[q, at(xy_rows, 32)], along_y(d))
-                b = (full.at[q, at(yx_rows, 32)], full.at[q, at(yx_rows, 32)], along_x(d))
-                ss, rs = s5, q5
+                found.append((full.at[q, at(xy_rows, 32)], full.at[q, at(xy_rows, 32)], along_y[d]))
+                found.append((full.at[q, at(yx_rows, 32)], full.at[q, at(yx_rows, 32)], along_x[d]))
             else:
-                a = (full.at[q, at(x_rows, 128)], full.at[q, at(x_rows, 128)], along_x(d))
-                b = (full.at[q, at(y_rows, 128)], full.at[q, at(y_rows, 128)], along_y(d))
-                ss, rs = s6, q6
-            for i, (src, dst, peer) in enumerate((a, b)):
-                found.append(remote(src, dst, ss.at[q, i * 3 + d - 1], rs.at[q, i * 3 + d - 1], peer))
+                found.append((full.at[q, at(x_rows, 128)], full.at[q, at(x_rows, 128)], along_x[d]))
+                found.append((full.at[q, at(y_rows, 128)], full.at[q, at(y_rows, 128)], along_y[d]))
         return found
 
     def go(level, q):
-        for copy in copies(level, q):
-            copy.start()
+        for src, dst, peer in copies(level, q):
+            remote(src, dst, level_send.at[level, q], level_recv.at[level, q], peer).start()
+
+    def wait_all(level, q, sem):
+        whole = (r0, r1, r2, r3)[level].at[q] if level < 4 else full.at[q, pl.ds(0, (56, 192, 768, 1024)[level - 4])]
+        pltpu.make_async_copy(whole, whole, sem).wait()
 
     def arrived(level, q):
-        for copy in copies(level, q):
-            copy.wait_recv()
+        wait_all(level, q, level_recv.at[level, q])
+
+    def left_here(level, q):
+        wait_all(level, q, level_send.at[level, q])
 
     def step(level, q):
         arrived(level - 1, q)
+        if level >= 2:
+            left_here(level - 2, q)
         if level == 1:
             mine = at(c * 1024, 1024)
             g[q, mine] = g[q, mine] + r0[q]
@@ -259,46 +247,47 @@
         lanes = at(hp * LANES, LANES)
         first = lax.broadcasted_iota(jnp.int32, (WIN, LANES), 1) < HD
         sums_k, sums_v, mixed_ts, dq_ts = [], [], [], []
+        heads = []
         for half in range(2):
             h = hp * 2 + half
-            own = at(h * LANES, LANES)
             double = at(h * 2 * LANES, 2 * LANES)
-            k_h, v_h = kp[:, own], vp[:, own]
+            k_h, v_h = kp[:, at(h * LANES, LANES)], vp[:, at(h * LANES, LANES)]
             q_h, do_h = qp[:, double], dop[:, double]
             scores = dot(jnp.concatenate([k_h, k_h], axis=1), q_h, NT) + bias[...]
+            d_prob = dot(jnp.concatenate([v_h, v_h], axis=1), do_h, NT)
+            heads.append((h, q_h[:, :LANES], do_h[:, :LANES], scores, d_prob))
+        probs = []
+        for h, q_hl, do_hl, scores, d_prob in heads:
             weights = jnp.exp(scores - jnp.max(scores, axis=0, keepdims=True))
             prob = weights * (1.0 / jnp.sum(weights, axis=0, keepdims=True))
             p_high, p_low = split(prob)
-            v_t = vt[own]
+            v_t = vt[at(h * LANES, LANES)]
             both = dot(v_t, p_high) + dot(v_t, p_low)
             mixed_t = both[:HD] + both[HD:]
             mixed_ts.append(mixed_t)
-            do_hl = do_h[:, :LANES]
             sum_v = dot(p_high, do_hl) + dot(p_low, do_hl)
             sums_v.append(sum_v + pltpu.roll(sum_v, HD, 1))
-            d_prob = dot(jnp.concatenate([v_h, v_h], axis=1), do_h, NT)
+            probs.append(prob)
+        for (h, q_hl, do_hl, scores, d_prob), prob, mixed_t in zip(heads, probs, mixed_ts):
             inner = jnp.sum(mixed_t * do_t[at(h * HD, HD)], axis=0, keepdims=True)
             ds_high, ds_low = split(prob * (d_prob - inner))
-            k_t = kt[own]
+            k_t = kt[at(h * LANES, LANES)]
             both = dot(k_t, ds_high) + dot(k_t, ds_low)
             dq_ts.append((both[:HD] + both[HD:]) * HD**-0.5)
-            q_hl = q_h[:, :LANES]
             sum_k = dot(ds_high, q_hl) + dot(ds_low, q_hl)
             sums_k.append(sum_k + pltpu.roll(sum_k, HD, 1))
-            if half == 0:
-
-                @pl.when(hp >= 1)
-                def _():
-                    step(1, hp - 1)
-
         dk_pair = put(dk2, jnp.where(first, sums_k[0], sums_k[1]), ALL, lanes)
         dv_pair = put(dv2, jnp.where(first, sums_v[0], sums_v[1]), ALL, lanes)
         dq_pair = put(dq2, jnp.concatenate(dq_ts, axis=0).T, ALL, lanes)
+        @pl.when(hp >= 1)
+        def _():
+            step(1, hp - 1)
+
         mixed_t = jnp.concatenate(mixed_ts, axis=0)
         put(o2, mixed_t.T, ALL, lanes)
         kv = tuple(jnp.concatenate([a, b], axis=1) for a, b in zip(dk_pair, dv_pair))
         grad_kv = dot3(pair(hid_t, ALL, ALL), kv)
-        g[hp, :D] = dot3(pair(hid_t, ALL, slice(ROWS, 2 * ROWS)), dq_pair)
+        g[hp, :D] = dot3(pair(hid_t, ALL, slice(0, ROWS)), dq_pair)
         g[hp, D : 2 * D] = grad_kv[:, :LANES]
         g[hp, 2 * D : 3 * D] = grad_kv[:, LANES:]
         grad_o = dot3(split(mixed_t), pair(cot2, ALL, ALL))
@@ -315,7 +304,7 @@
         rows = slice(block * ROWS, (block + 1) * ROWS)
         part = dot3(pair(dk2, rows, ALL), pair(w2.at[1], ALL, ALL), NT)
         part = part + dot3(pair(dv2, rows, ALL), pair(w2.at[2], ALL, ALL), NT)
-        if block == 1:
+        if block == 0:
             part = part + dot3(pair(dq2, ALL, ALL), pair(w2.at[0], ALL, ALL), NT)
         grad = part * gain_row
         hat = xhat[rows]
@@ -323,8 +312,8 @@
         return rstd[rows] * (grad - jnp.mean(grad, axis=1, keepdims=True) - hat * inner)
 
     back = [
-        remote(dhalo.at[0], halo_in.at[1], dh_send.at[0], dh_recv.at[0], before),
-        remote(dhalo.at[1], halo_in.at[0], dh_send.at[1], dh_recv.at[1], after),
+        remote(dhalo.at[0], halo_in.at[0], dh_send.at[0], dh_recv.at[0], partner),
+        remote(dhalo.at[1], halo_in.at[1], dh_send.at[1], dh_recv.at[1], other),
     ]
     outs = []
 
@@ -348,7 +337,7 @@
             full[q, :D] * wf[0, :, lanes] + full[q, D : 2 * D] * wf[1, :, lanes] + full[q, 2 * D : 3 * D] * wf[2, :, lanes]
         )
 
-    dhalo[0] = d_hidden(0)
+    dhalo[0] = d_hidden(1)
     step(1, 3)
     step(2, 2)
     step(3, 1)
@@ -358,12 +347,12 @@
     step(2, 3)
     step(4, 1)
     step(5, 0)
-    dtok_buf[...] = d_hidden(1) + cotf[...]
+    dtok_buf[...] = d_hidden(0) + cotf[...]
     step(3, 3)
     step(4, 2)
     step(5, 1)
     step(6, 0)
-    res_buf[...] = dot3(pair(o2, ALL, ALL), pair(w2.at[3], ALL, ALL)) + xwin[ROWS : 2 * ROWS]
+    res_buf[...] = dot3(pair(o2, ALL, ALL), pair(w2.at[3], ALL, ALL)) + xwin[:ROWS]
     write(res_buf, result, out_sem.at[0])
     dg_acc[...] = jnp.zeros_like(dg_acc)
     step(4, 3)
@@ -387,14 +376,13 @@
     finish(2)
     finish(3)
     d_gain[...] = jnp.sum(dg_acc[...].T, axis=0, keepdims=True) / gain_row
-    to_after.wait_send()
-    to_before.wait_send()
+    to_far.wait_send()
+    to_near.wait_send()
     for copy in back:
         copy.wait_send()
     for q in range(QUARTERS):
-        for level in range(8):
-            for copy in copies(level, q):
-                copy.wait_send()
+        left_here(6, q)
+        left_here(7, q)
     for copy in outs:
         copy.wait()
 
@@ -445,8 +433,7 @@
         dma((2,)),
         dma((2,)),
     ]
-    for peers in ((4,), (4, 6), (4, 6), (4, 7), (4, 7), (4, 6), (4, 6), (4,)):
-        scratch += [dma(peers), dma(peers)]
+    scratch += [dma((8, QUARTERS)), dma((8, QUARTERS))]
     scratch += [dma((2,)), dma((2,)), dma((30,))]
     return pl.pallas_call(
         kernel,

time: 91.9 us -> 85.3 us (0.928)
  Pallas kernels: 91 us -> 84.4 us
    pallas_call x1, Pallas kernels: 86 us -> 79.4 us  [layer(): pl.pallas_call(kernel, out_shape=(shape((ROWS, D), F32), shape((ROWS, D),...]
where the time goes in v4:
time: 85.3 us; the launch traced here: 85.2 us
  Pallas kernels  84.4 us (99%)
    pallas_call x1, Pallas kernels, layer(): pl.pallas_call(kernel, out_shape=(shape((ROWS, D), F32), shape((ROWS, D),...  79.4 us
    pallas_call x1, Pallas kernels, written(): pl.pallas_call(write_kernel, out_shape=tuple((jax.ShapeDtypeStruct(a.shap...  5.08 us

profile of v4, /device:TPU:1, one launch (start us, length us, event | category | flops | bytes accessed | tf_op | source)
XLA Modules:
  0.0 85.2 jit_solution(12728198282959732152)
XLA Ops:
  0.6 79.4 %patch_layer.1 = (f32[256,512]{1,0:T(8,128)}, f32[256,512]{1,0:T(8,128)}, f32[1,512]{1,0:T(1,128)}, f32[512,512]{1,0:T(8,128)}, f32[512,512]{1,0:T(8,128)}, /*index=5*/f32[512,512]{1,0:T(8,128)}, f32[512,512]{1,0:T(8,128)}) custom-call(s32[2,3]{1,0:T(2,128)} %nlist.1, s32[2]{0:T(128)} %ncount.1, f32[256,512]{1,0:T(8,128)} %tok.1, f32[1,512]{1,0:T(1,128)} %bitcast.2, ...), custom_call_target="tpu_custom_call" | custom-call | tf_op jit(solution)/shard_map/patch_layer/pallas_call | solution.py:438
  80.0 5.1 %write_results.1 = (f32[256,512]{1,0:T(8,128)}, f32[256,512]{1,0:T(8,128)}, f32[1,512]{1,0:T(1,128)}, f32[512,512]{1,0:T(8,128)}, f32[512,512]{1,0:T(8,128)}, /*index=5*/f32[512,512]{1,0:T(8,128)}, f32[512,512]{1,0:T(8,128)}) custom-call(f32[256,512]{1,0:T(8,128)} %get-tuple-element.21.refs_0_, f32[256,512]{1,0:T(8,128)} %get-tuple-element.22.refs_1_, ...), custom_call_target="tpu_custom_call" | custom-call | tf_op jit(solution)/shard_map/write_results/pallas_call | solution.py:486

commit v5 on v4

--- a/solution.py
+++ b/solution.py
@@ -71,10 +71,10 @@
 
 def kernel(
     nlist, ncount, tok, gain, wq, wk, wv, wo, cot,
-    result, d_tokens, d_gain, d_q, d_k, d_v, d_o,
+    full, res_buf, dtok_buf, d_gain,
     xwin, wf, cotf, xhat, rstd, hid_t, w2, cot2, kp, vp, kt, vt, qp, dop, do_t, bias, dk2, dv2, dq2, o2,
-    g, r0, r1, acc2, r2, acc3, r3, full, dhalo, halo_in, res_buf, dtok_buf, dg_acc,
-    load_sem, tok_send, tok_recv, level_send, level_recv, dh_send, dh_recv, out_sem,
+    g, r0, r1, acc2, r2, acc3, r3, dhalo, halo_in, dg_acc,
+    load_sem, tok_send, tok_recv, level_send, level_recv, dh_send, dh_recv,
 ):
     s = lax.axis_index("space")
     y = lax.axis_index("slab")
@@ -315,24 +315,9 @@
         remote(dhalo.at[0], halo_in.at[0], dh_send.at[0], dh_recv.at[0], partner),
         remote(dhalo.at[1], halo_in.at[1], dh_send.at[1], dh_recv.at[1], other),
     ]
-    outs = []
-
-    def write(src, dst, sem):
-        copy = pltpu.make_async_copy(src, dst, sem)
-        copy.start()
-        outs.append(copy)
-
     def finish(q):
         arrived(7, q)
         lanes = slice(q * LANES, (q + 1) * LANES)
-        for i, ref in enumerate((d_q, d_k, d_v)):
-            write(full.at[q, pl.ds(i * D, D)], ref.at[:, pl.ds(q * LANES, LANES)], out_sem.at[2 + q * 7 + i])
-        for i in range(4):
-            write(
-                full.at[q, pl.ds(3 * D + i * LANES, LANES)],
-                d_o.at[pl.ds(q * LANES, LANES), pl.ds(i * LANES, LANES)],
-                out_sem.at[2 + q * 7 + 3 + i],
-            )
         dg_acc[...] += (
             full[q, :D] * wf[0, :, lanes] + full[q, D : 2 * D] * wf[1, :, lanes] + full[q, 2 * D : 3 * D] * wf[2, :, lanes]
         )
@@ -353,7 +338,6 @@
     step(5, 1)
     step(6, 0)
     res_buf[...] = dot3(pair(o2, ALL, ALL), pair(w2.at[3], ALL, ALL)) + xwin[:ROWS]
-    write(res_buf, result, out_sem.at[0])
     dg_acc[...] = jnp.zeros_like(dg_acc)
     step(4, 3)
     step(5, 2)
@@ -371,7 +355,6 @@
     for copy in back:
         copy.wait_recv()
     dtok_buf[...] = dtok_buf[...] + (halo_in[0] + halo_in[1])
-    write(dtok_buf, d_tokens, out_sem.at[1])
     step(7, 3)
     finish(2)
     finish(3)
@@ -383,8 +366,6 @@
     for q in range(QUARTERS):
         left_here(6, q)
         left_here(7, q)
-    for copy in outs:
-        copy.wait()
 
 
 def layer(nlist, ncount, tokens, gain, wq, wk, wv, wo, cot):
@@ -423,75 +404,58 @@
         v((4, 2, 3, 32, LANES), F32),
         v((4, 64, LANES), F32),
         v((4, 7, 8, LANES), F32),
-        v((4, 2048, LANES), F32),
         v((2, ROWS, D), F32),
         v((2, ROWS, D), F32),
-        v((ROWS, D), F32),
-        v((ROWS, D), F32),
         v((D, LANES), F32),
         dma((6,)),
         dma((2,)),
         dma((2,)),
     ]
     scratch += [dma((8, QUARTERS)), dma((8, QUARTERS))]
-    scratch += [dma((2,)), dma((2,)), dma((30,))]
+    scratch += [dma((2,)), dma((2,))]
     return pl.pallas_call(
         kernel,
-        out_shape=(
-            shape((ROWS, D), F32),
-            shape((ROWS, D), F32),
-            shape((1, D), F32),
-            shape((D, D), F32),
-            shape((D, D), F32),
-            shape((D, D), F32),
-            shape((D, D), F32),
-        ),
+        out_shape=(v((QUARTERS, 2048, LANES), F32), v((ROWS, D), F32), v((ROWS, D), F32), v((1, D), F32)),
         in_specs=[smem] * 2 + [hbm, vmem] + [hbm] * 5,
-        out_specs=(hbm, hbm, vmem, hbm, hbm, hbm, hbm),
+        out_specs=(vmem,) * 4,
         scratch_shapes=scratch,
         compiler_params=pltpu.CompilerParams(
-            collective_id=0, has_side_effects=True, vmem_limit_bytes=60 << 20
+            collective_id=0, has_side_effects=True, vmem_limit_bytes=52 << 20
         ),
         name="patch_layer",
     )(nlist, ncount, tokens, gain, wq, wk, wv, wo, cot)
 
 
-PARTS = 4
-
-
-def write_kernel(*refs):
-    arrays = (len(refs) - 2) // 3
-    load_sem, store_sem = refs[-2:]
-    loads, stores = [], []
-    for i in range(arrays):
-        src, dst, buf = refs[i], refs[arrays + i], refs[2 * arrays + i]
-        rows = src.shape[0]
-        parts = PARTS if rows >= 8 * PARTS else 1
-        for j in range(parts):
-            block = pl.ds(j * (rows // parts), rows // parts)
-            loads.append(pltpu.make_async_copy(src.at[block], buf.at[block], load_sem.at[i, j]))
-            stores.append(pltpu.make_async_copy(buf.at[block], dst.at[block], store_sem.at[i, j]))
-    for load in loads:
-        load.start()
-    for load, store in zip(loads, stores):
-        load.wait()
-        store.start()
-    for store in stores:
-        store.wait()
-
-
-def written(*arrays):
+def write_kernel(full, res, dtok, gain, result, d_tokens, d_gain, d_q, d_k, d_v, d_o, sem):
+    pairs = [(res, result), (dtok, d_tokens), (gain, d_gain)]
+    for q in range(QUARTERS):
+        lanes = pl.ds(q * LANES, LANES)
+        for i, ref in enumerate((d_q, d_k, d_v)):
+            pairs.append((full.at[q, pl.ds(i * D, D)], ref.at[:, lanes]))
+        for i in range(4):
+            pairs.append((full.at[q, pl.ds(3 * D + i * LANES, LANES)], d_o.at[lanes, pl.ds(i * LANES, LANES)]))
+    copies = [pltpu.make_async_copy(src, dst, sem.at[i]) for i, (src, dst) in enumerate(pairs)]
+    for copy in copies:
+        copy.start()
+    for copy in copies:
+        copy.wait()
+
+
+def written(full, res, dtok, gain):
+    shape = jax.ShapeDtypeStruct
     hbm = pl.BlockSpec(memory_space=pl.ANY)
-    sems = pltpu.SemaphoreType.DMA((len(arrays), PARTS))
+    vmem = pl.BlockSpec(memory_space=pltpu.VMEM)
+    rows, row, square = shape((ROWS, D), F32), shape((1, D), F32), shape((D, D), F32)
+    held = [pltpu.with_memory_space_constraint(a, pltpu.VMEM) for a in (full, res, dtok, gain)]
     return pl.pallas_call(
         write_kernel,
-        out_shape=tuple(jax.ShapeDtypeStruct(a.shape, a.dtype) for a in arrays),
-        in_specs=[hbm] * len(arrays),
-        out_specs=(hbm,) * len(arrays),
-        scratch_shapes=[pltpu.VMEM(a.shape, a.dtype) for a in arrays] + [sems, sems],
-        compiler_params=pltpu.CompilerParams(vmem_limit_bytes=60 << 20),
+        out_shape=(rows, rows, row, square, square, square, square),
+        in_specs=[vmem] * 4,
+        out_specs=(hbm,) * 7,
+        scratch_shapes=[pltpu.SemaphoreType.DMA((3 + 7 * QUARTERS,))],
+        compiler_params=pltpu.CompilerParams(vmem_limit_bytes=8 << 20),
         name="write_results",
-    )(*arrays)
+    )(*held)
 
 
 def body(tokens, gain, wq, wk, wv, wo, nlist, ncount, cot):

time: 85.3 us -> 81.1 us (0.951)
  Pallas kernels: 84.4 us -> 80.2 us
    pallas_call x2, Pallas kernels: 84.4 us -> 80.2 us  [the longest x1 77.6 us: layer(): pl.pallas_call(kernel, out_shape=(v((QUARTERS, 2048, LANES), F32), v((ROW...]
where the time goes in v5:
time: 81.1 us; the launch traced here: 81 us
  Pallas kernels  80.2 us (99%)
    pallas_call x1, Pallas kernels, layer(): pl.pallas_call(kernel, out_shape=(v((QUARTERS, 2048, LANES), F32), v((ROW...  77.6 us
    pallas_call x1, Pallas kernels, written(): pl.pallas_call(write_kernel, out_shape=(rows, rows, row, square, square,...  2.58 us

profile of v5, /device:TPU:1, one launch (start us, length us, event | category | flops | bytes accessed | tf_op | source)
XLA Modules:
  0.0 81.0 jit_solution(4658753813699342159)
XLA Ops:
  0.6 77.6 %patch_layer.1 = (f32[4,2048,128]{2,1,0:T(8,128)S(1)}, f32[256,512]{1,0:T(8,128)S(1)}, f32[256,512]{1,0:T(8,128)S(1)}, f32[1,512]{1,0:T(1,128)S(1)}) custom-call(s32[2,3]{1,0:T(2,128)} %nlist.1, s32[2]{0:T(128)} %ncount.1, f32[256,512]{1,0:T(8,128)} %tok.1, f32[1,512]{1,0:T(1,128)} %bitcast.2, f32[512,512]{1,0:T(8,128)} %wq.1, f32[512,512]{1,0:T(8,128)} %wk.1, ...), custom_call_target="tpu_custom_call" | custom-call | tf_op jit(solution)/shard_map/patch_layer/pallas_call | solution.py:416
  78.3 2.6 %write_results.1 = (f32[256,512]{1,0:T(8,128)}, f32[256,512]{1,0:T(8,128)}, f32[1,512]{1,0:T(1,128)}, f32[512,512]{1,0:T(8,128)}, f32[512,512]{1,0:T(8,128)}, /*index=5*/f32[512,512]{1,0:T(8,128)}, f32[512,512]{1,0:T(8,128)}) custom-call(f32[4,2048,128]{2,1,0:T(8,128)S(1)} %get-tuple-element.18.full, f32[256,512]{1,0:T(8,128)S(1)} %get-tuple-element.19.res, ...), custom_call_target="tpu_custom_call" | custom-call | tf_op jit(solution)/shard_map/write_results/pallas_call | solution.py:450

commit v6 on v5

--- a/solution.py
+++ b/solution.py
@@ -17,6 +17,8 @@
 NX, NY, NZ = 4, 4, 8
 QUARTERS = 4
 LANES = 128
+FAR = (2, 1, 3)
+FAR_Z = (4, 3, 5, 2, 6, 1, 7)
 
 NN = (((1,), (0,)), ((), ()))
 NT = (((1,), (1,)), ((), ()))
@@ -97,7 +99,7 @@
         load.start()
 
     barrier = pltpu.get_barrier_semaphore()
-    everyone = [partner, other] + along_x[1:] + along_y[1:] + along_z[1:]
+    everyone = [along_z[d] for d in FAR_Z] + [along_x[d] for d in FAR] + [along_y[d] for d in FAR] + [other, partner]
     for peer in everyone:
         pl.semaphore_signal(barrier, inc=1, device_id=peer, device_id_type=MESH)
     pl.semaphore_wait(barrier, len(everyone))
@@ -189,9 +191,9 @@
         if level == 7:
             return [(full.at[q, at(c * 1024, 1024)], full.at[q, at(c * 1024, 1024)], partner)]
         if level == 3:
-            return [(acc3.at[q, at(zs[d] * 8, 8)], r3.at[q, d - 1], along_z[d]) for d in range(1, NZ)]
+            return [(acc3.at[q, at(zs[d] * 8, 8)], r3.at[q, d - 1], along_z[d]) for d in FAR_Z]
         if level == 4:
-            return [(full.at[q, at(tile, 8)], full.at[q, at(tile, 8)], along_z[d]) for d in range(1, NZ)]
+            return [(full.at[q, at(tile, 8)], full.at[q, at(tile, 8)], along_z[d]) for d in FAR_Z]
         found = []
         for d in range(1, 4):
             if level == 1:
@@ -352,10 +354,10 @@
     finish(0)
     step(7, 2)
     finish(1)
+    step(7, 3)
     for copy in back:
         copy.wait_recv()
     dtok_buf[...] = dtok_buf[...] + (halo_in[0] + halo_in[1])
-    step(7, 3)
     finish(2)
     finish(3)
     d_gain[...] = jnp.sum(dg_acc[...].T, axis=0, keepdims=True) / gain_row

time: 81.1 us -> 80.8 us (level)
  no operation moved by 1% of the time
where the time goes in v6:
time: 80.8 us; the launch traced here: 80.7 us
  Pallas kernels  79.9 us (99%)
    pallas_call x1, Pallas kernels, layer(): pl.pallas_call(kernel, out_shape=(v((QUARTERS, 2048, LANES), F32), v((ROW...  77.3 us
    pallas_call x1, Pallas kernels, written(): pl.pallas_call(write_kernel, out_shape=(rows, rows, row, square, square,...  2.58 us

profile of v6, /device:TPU:1, one launch (start us, length us, event | category | flops | bytes accessed | tf_op | source)
XLA Modules:
  0.0 80.7 jit_solution(13031315382220795395)
XLA Ops:
  0.6 77.3 %patch_layer.1 = (f32[4,2048,128]{2,1,0:T(8,128)S(1)}, f32[256,512]{1,0:T(8,128)S(1)}, f32[256,512]{1,0:T(8,128)S(1)}, f32[1,512]{1,0:T(1,128)S(1)}) custom-call(s32[2,3]{1,0:T(2,128)} %nlist.1, s32[2]{0:T(128)} %ncount.1, f32[256,512]{1,0:T(8,128)} %tok.1, f32[1,512]{1,0:T(1,128)} %bitcast.2, f32[512,512]{1,0:T(8,128)} %wq.1, f32[512,512]{1,0:T(8,128)} %wk.1, ...), custom_call_target="tpu_custom_call" | custom-call | tf_op jit(solution)/shard_map/patch_layer/pallas_call | solution.py:418
  77.9 2.6 %write_results.1 = (f32[256,512]{1,0:T(8,128)}, f32[256,512]{1,0:T(8,128)}, f32[1,512]{1,0:T(1,128)}, f32[512,512]{1,0:T(8,128)}, f32[512,512]{1,0:T(8,128)}, /*index=5*/f32[512,512]{1,0:T(8,128)}, f32[512,512]{1,0:T(8,128)}) custom-call(f32[4,2048,128]{2,1,0:T(8,128)S(1)} %get-tuple-element.18.full, f32[256,512]{1,0:T(8,128)S(1)} %get-tuple-element.19.res, ...), custom_call_target="tpu_custom_call" | custom-call | tf_op jit(solution)/shard_map/write_results/pallas_call | solution.py:452
